TPU v7x, 32 devices: a whole 2x2x4 slice. The times are simulated.
32 devices in a mesh: pipe: 2 (over x), dp: 4 (over z), mp: 4 (over y, core).
Axes of the slice: x: 2, y: 2, z: 4, core: 2. Of those that a mesh axis runs over, the one named last changes fastest.
Arguments:
- section_in: bfloat16 [2, 12, 729, 1152], P('pipe', 'dp'), may hold values from -6 to 6
- ln1_gain: bfloat16 [2, 1152], P('pipe'), may hold values from 0.099609375 to 1.8984375
- ln1_bias: bfloat16 [2, 1152], P('pipe'), may hold values from -3 to 3
- qkv_weight: bfloat16 [2, 1152, 3, 1152], P('pipe', None, None, 'mp'), may hold values from -0.1875 to 0.1875
- qv_bias: bfloat16 [2, 2, 1152], P('pipe', None, 'mp'), may hold values from -3 to 3
- out_weight: bfloat16 [2, 1152, 1152], P('pipe', 'mp'), may hold values from -3 to 3
- out_bias: bfloat16 [2, 1152], P('pipe'), may hold values from -3 to 3
- ln2_gain: bfloat16 [2, 1152], P('pipe'), may hold values from 0.099609375 to 1.8984375
- ln2_bias: bfloat16 [2, 1152], P('pipe'), may hold values from -3 to 3
- fc1_weight: bfloat16 [2, 1152, 4304], P('pipe', None, 'mp'), may hold values from -0.1875 to 0.1875
- fc1_bias: bfloat16 [2, 4304], P('pipe', 'mp'), may hold values from -3 to 3
- fc2_weight: bfloat16 [2, 4304, 1152], P('pipe', 'mp'), may hold values from -0.1875 to 0.1875
- fc2_bias: bfloat16 [2, 1152], P('pipe'), may hold values from -4 to 4
Outputs:
- section_out: bfloat16 [2, 12, 729, 1152], P('pipe', 'dp')
- grad_ln1_gain: float32 [2, 1152], P('pipe')
- grad_ln1_bias: float32 [2, 1152], P('pipe')
- grad_qkv_weight: float32 [2, 1152, 3, 1152], P('pipe', None, None, 'mp')
- grad_qv_bias: float32 [2, 2, 1152], P('pipe', None, 'mp')
- grad_out_weight: float32 [2, 1152, 1152], P('pipe', 'mp')
- grad_out_bias: float32 [2, 1152], P('pipe')
- grad_ln2_gain: float32 [2, 1152], P('pipe')
- grad_ln2_bias: float32 [2, 1152], P('pipe')
- grad_fc1_weight: float32 [2, 1152, 4304], P('pipe', None, 'mp')
- grad_fc1_bias: float32 [2, 4304], P('pipe', 'mp')
- grad_fc2_weight: float32 [2, 4304, 1152], P('pipe', 'mp')
- grad_fc2_bias: float32 [2, 1152], P('pipe')
All inputs are finite; a program needn't handle non-finite values.
Results may differ from a plain program's by a relative error of at most 0.028.
Values may be sent and summed in bfloat16 or wider, within the bound.
A program may use at most 320 MiB of HBM per device.

v0:
```python
import jax
import jax.numpy as jnp
from jax import lax
from jax.sharding import PartitionSpec as P

HDIM = 72


EPSILON = 1e-06
GELU_SCALE = 0.7978845608028654
GELU_CUBIC = 0.044715


def shifted(value, axis, by):
    peers = lax.axis_size(axis)
    pairs = [(i, i + by) for i in range(peers) if 0 <= i + by < peers]
    return lax.ppermute(value, axis, pairs)


def norm_rows(values, gain_vec, shift_vec):
    center = values - jnp.mean(values, axis=-1, keepdims=True)
    inv_std = lax.rsqrt(jnp.mean(center * center, axis=-1, keepdims=True) + EPSILON)
    x_hat = center * inv_std
    return (x_hat * gain_vec + shift_vec, x_hat, inv_std)


def norm_back(d_out, x_hat, inv_std, gain_vec):
    d_hat = d_out * gain_vec
    inner = (
        d_hat
        - jnp.mean(d_hat, axis=-1, keepdims=True)
        - x_hat * jnp.mean(d_hat * x_hat, axis=-1, keepdims=True)
    )
    return (inv_std * inner, jnp.sum(d_out * x_hat, axis=0), jnp.sum(d_out, axis=0))


def gelu_parts(pre_act):
    tanh_val = jnp.tanh(GELU_SCALE * (pre_act + GELU_CUBIC * pre_act * pre_act * pre_act))
    act_value = 0.5 * pre_act * (1.0 + tanh_val)
    act_slope = 0.5 * (1.0 + tanh_val) + 0.5 * pre_act * (
        1.0 - tanh_val * tanh_val
    ) * GELU_SCALE * (1.0 + 3.0 * GELU_CUBIC * pre_act * pre_act)
    return (act_value, act_slope)


def attend(query, key_rows, value_rows, scaling):
    scores = (
        jnp.einsum("qhd,khd->hqk", query, key_rows, preferred_element_type=jnp.float32) * scaling
    )
    row_max = jnp.max(scores, axis=-1, keepdims=True)
    exp_terms = jnp.exp(scores - row_max)
    row_total = jnp.sum(exp_terms, axis=-1, keepdims=True)
    attn_probs = (exp_terms / row_total).astype(jnp.bfloat16)
    mixed = jnp.einsum("hqk,khd->qhd", attn_probs, value_rows, preferred_element_type=jnp.float32)
    return (mixed, row_max + jnp.log(row_total))


def attend_back(query, key_rows, value_rows, log_total, d_mixed, scaling):
    scores = (
        jnp.einsum("qhd,khd->hqk", query, key_rows, preferred_element_type=jnp.float32) * scaling
    )
    attn_probs = jnp.exp(scores - log_total)
    probs_low = attn_probs.astype(jnp.bfloat16)
    d_values = jnp.einsum("hqk,qhd->khd", probs_low, d_mixed, preferred_element_type=jnp.float32)
    d_probs = jnp.einsum("qhd,khd->hqk", d_mixed, value_rows, preferred_element_type=jnp.float32)
    inner = jnp.sum(d_probs * attn_probs, axis=-1, keepdims=True)
    d_scores = (attn_probs * (d_probs - inner)).astype(jnp.bfloat16)
    d_query = (
        jnp.einsum("hqk,khd->qhd", d_scores, key_rows, preferred_element_type=jnp.float32) * scaling
    )
    d_keys = (
        jnp.einsum("hqk,qhd->khd", d_scores, query, preferred_element_type=jnp.float32) * scaling
    )
    return (
        d_query.astype(jnp.bfloat16),
        d_keys.astype(jnp.bfloat16),
        d_values.astype(jnp.bfloat16),
    )


def attention_part(residual, gain_one, shift_one, w_qkv, bias_qv, scaling):
    row_count = residual.shape[0]
    normed = norm_rows(residual, gain_one, shift_one)[0]
    packed = jnp.dot(
        normed.astype(jnp.bfloat16), w_qkv, preferred_element_type=jnp.float32
    ).reshape(row_count, 3, -1)
    bias_three = jnp.stack([bias_qv[0], jnp.zeros_like(bias_qv[0]), bias_qv[1]])
    packed = (packed + bias_three).astype(jnp.bfloat16)
    local_width = packed.shape[2]
    head_count = local_width // HDIM
    query = packed[:, 0].reshape(row_count, head_count, HDIM)
    key_rows = packed[:, 1].reshape(row_count, head_count, HDIM)
    value_rows = packed[:, 2].reshape(row_count, head_count, HDIM)
    mixed, log_total = attend(query, key_rows, value_rows, scaling)
    return (packed, log_total, mixed.reshape(row_count, local_width).astype(jnp.bfloat16))


def attention_back(packed, log_total, d_attn, mixed_low, w_out, scaling):
    row_count = packed.shape[0]
    local_width = packed.shape[2]
    head_count = local_width // HDIM
    grad_w_out = jnp.einsum("sc,sd->cd", mixed_low, d_attn, preferred_element_type=jnp.float32)
    d_mixed = jnp.einsum("sd,cd->sc", d_attn, w_out, preferred_element_type=jnp.float32).astype(
        jnp.bfloat16
    )
    query = packed[:, 0].reshape(row_count, head_count, HDIM)
    key_rows = packed[:, 1].reshape(row_count, head_count, HDIM)
    value_rows = packed[:, 2].reshape(row_count, head_count, HDIM)
    d_query, d_keys, d_values = attend_back(
        query,
        key_rows,
        value_rows,
        log_total,
        d_mixed.reshape(row_count, head_count, HDIM),
        scaling,
    )
    d_query = d_query.reshape(row_count, local_width)
    d_values = d_values.reshape(row_count, local_width)
    d_packed = jnp.stack(
        [d_query, d_keys.reshape(row_count, local_width), d_values], axis=1
    ).reshape(row_count, 3 * local_width)
    grad_bias_qv = jnp.stack(
        [
            jnp.sum(d_query.astype(jnp.float32), axis=0),
            jnp.sum(d_values.astype(jnp.float32), axis=0),
        ]
    )
    return (grad_w_out, d_packed, grad_bias_qv)


def layer_forward(inputs, weights, scaling):
    (
        gain_one,
        shift_one,
        w_qkv,
        bias_qv,
        w_out,
        bias_out,
        gain_two,
        shift_two,
        w_fc1,
        bias_fc1,
        w_fc2,
        bias_fc2,
    ) = weights
    residual = inputs.astype(jnp.float32)
    packed, log_total, mixed_low = attention_part(
        residual, gain_one, shift_one, w_qkv, bias_qv, scaling
    )
    branch = lax.psum(
        jnp.dot(mixed_low, w_out, preferred_element_type=jnp.float32).astype(jnp.bfloat16), "mp"
    ).astype(jnp.float32)
    mid_stream = residual + branch + bias_out
    normed_two = norm_rows(mid_stream, gain_two, shift_two)[0]
    pre_act = (
        jnp.dot(normed_two.astype(jnp.bfloat16), w_fc1, preferred_element_type=jnp.float32)
        + bias_fc1
    )
    act_out = gelu_parts(pre_act)[0]
    branch_two = lax.psum(
        jnp.dot(act_out.astype(jnp.bfloat16), w_fc2, preferred_element_type=jnp.float32).astype(
            jnp.bfloat16
        ),
        "mp",
    ).astype(jnp.float32)
    layer_out = (mid_stream + branch_two + bias_fc2).astype(jnp.bfloat16)
    kept_state = (inputs, packed, log_total, mixed_low, mid_stream)
    return (layer_out, kept_state)


def layer_backward(kept_state, d_out, weights, scaling):
    (
        gain_one,
        shift_one,
        w_qkv,
        bias_qv,
        w_out,
        bias_out,
        gain_two,
        shift_two,
        w_fc1,
        bias_fc1,
        w_fc2,
        bias_fc2,
    ) = weights
    inputs, packed, log_total, mixed_low, mid_stream = (
        kept_state[0],
        kept_state[1],
        kept_state[2],
        kept_state[3],
        kept_state[4],
    )
    residual = inputs.astype(jnp.float32)
    normed, hat_one, std_one = norm_rows(residual, gain_one, shift_one)
    normed_two, hat_two, std_two = norm_rows(mid_stream, gain_two, shift_two)
    normed_two_low = normed_two.astype(jnp.bfloat16)
    pre_act = jnp.dot(normed_two_low, w_fc1, preferred_element_type=jnp.float32) + bias_fc1
    act_out, act_slope = gelu_parts(pre_act)
    act_low = act_out.astype(jnp.bfloat16)
    grad_b_two = jnp.sum(d_out, axis=0)
    d_mlp = d_out.astype(jnp.bfloat16)
    grad_w_two = jnp.einsum("sf,sd->fd", act_low, d_mlp, preferred_element_type=jnp.float32)
    d_act = jnp.einsum("sd,fd->sf", d_mlp, w_fc2, preferred_element_type=jnp.float32)
    d_pre = (d_act * act_slope).astype(jnp.bfloat16)
    grad_w_one = jnp.einsum("sd,sf->df", normed_two_low, d_pre, preferred_element_type=jnp.float32)
    grad_b_one = jnp.sum(d_pre.astype(jnp.float32), axis=0)
    d_norm_two = lax.psum(
        jnp.einsum("sf,df->sd", d_pre, w_fc1, preferred_element_type=jnp.float32).astype(
            jnp.bfloat16
        ),
        "mp",
    ).astype(jnp.float32)
    d_mid_norm, grad_gain_two, grad_shift_two = norm_back(d_norm_two, hat_two, std_two, gain_two)
    d_mid = d_out + d_mid_norm
    grad_bias_out = jnp.sum(d_mid, axis=0)
    grad_w_out, d_packed, grad_bias_qv = attention_back(
        packed, log_total, d_mid.astype(jnp.bfloat16), mixed_low, w_out, scaling
    )
    grad_w_qkv = jnp.einsum(
        "sd,sc->dc", normed.astype(jnp.bfloat16), d_packed, preferred_element_type=jnp.float32
    )
    d_norm_one = lax.psum(
        jnp.einsum("sc,dc->sd", d_packed, w_qkv, preferred_element_type=jnp.float32).astype(
            jnp.bfloat16
        ),
        "mp",
    ).astype(jnp.float32)
    d_res_norm, grad_gain_one, grad_shift_one = norm_back(d_norm_one, hat_one, std_one, gain_one)
    d_input = (d_mid + d_res_norm).astype(jnp.bfloat16)
    grads = (
        grad_gain_one,
        grad_shift_one,
        grad_w_qkv,
        grad_bias_qv,
        grad_w_out,
        grad_bias_out,
        grad_gain_two,
        grad_shift_two,
        grad_w_one,
        grad_b_one,
        grad_w_two,
        grad_b_two,
    )
    return (d_input, grads)


def on_device(
    section_in,
    ln1_gain,
    ln1_bias,
    qkv_weight,
    qv_bias,
    out_weight,
    out_bias,
    ln2_gain,
    ln2_bias,
    fc1_weight,
    fc1_bias,
    fc2_weight,
    fc2_bias,
):
    section_pos = lax.axis_index("pipe")
    is_first = section_pos == 0
    feed_rows = section_in[0]
    micro_count = feed_rows.shape[0]
    model_width = feed_rows.shape[2]
    scaling = HDIM ** (-0.5)
    weights = (
        ln1_gain[0].astype(jnp.float32),
        ln1_bias[0].astype(jnp.float32),
        qkv_weight[0].reshape(model_width, -1),
        qv_bias[0].astype(jnp.float32),
        out_weight[0],
        out_bias[0].astype(jnp.float32),
        ln2_gain[0].astype(jnp.float32),
        ln2_bias[0].astype(jnp.float32),
        fc1_weight[0],
        fc1_bias[0].astype(jnp.float32),
        fc2_weight[0],
        fc2_bias[0].astype(jnp.float32),
    )

    def pick_side(low_side, high_side):
        return jnp.where(is_first, low_side, high_side)

    arriving = jnp.zeros(feed_rows.shape[1:], jnp.bfloat16)
    kept_ticks = []
    results = []
    for tick_num in range(micro_count + 1):
        pick_index = jnp.clip(tick_num - section_pos, 0, micro_count - 1)
        own_rows = lax.dynamic_index_in_dim(feed_rows, pick_index, 0, keepdims=False)
        layer_out, kept_state = layer_forward(
            jnp.where(is_first, own_rows, arriving), weights, scaling
        )
        kept_ticks.append(kept_state)
        results.append(layer_out)
        if tick_num < micro_count:
            arriving = shifted(layer_out, "pipe", 1)
    back_rows = jnp.zeros(feed_rows.shape[1:], jnp.bfloat16)
    totals = None
    sent_grads = []
    for tick_num in range(micro_count + 1):
        pick_index = jnp.clip(tick_num - 1 + section_pos, 0, micro_count - 1)
        own_rows = lax.dynamic_index_in_dim(feed_rows, pick_index, 0, keepdims=False)
        d_out = jnp.where(is_first, back_rows, own_rows).astype(jnp.float32)
        kept_state = jax.tree.map(
            pick_side, kept_ticks[max(tick_num - 1, 0)], kept_ticks[min(tick_num + 1, micro_count)]
        )
        d_input, grads = layer_backward(kept_state, d_out, weights, scaling)
        is_live = jnp.where(is_first, tick_num >= 1, tick_num < micro_count)
        grads = tuple((jnp.where(is_live, grad_item, 0.0) for grad_item in grads))
        totals = (
            grads
            if totals is None
            else tuple((left_item + right_item for left_item, right_item in zip(totals, grads)))
        )
        sent_grads.append(d_input)
        if tick_num < micro_count:
            back_rows = shifted(d_input, "pipe", -1)
    share_list = (
        lax.psum_scatter(
            totals[2].astype(jnp.bfloat16), "dp", scatter_dimension=0, tiled=True
        ).astype(jnp.float32),
        lax.psum_scatter(
            totals[4].astype(jnp.bfloat16), "dp", scatter_dimension=1, tiled=True
        ).astype(jnp.float32),
        lax.psum_scatter(
            totals[8].astype(jnp.bfloat16), "dp", scatter_dimension=0, tiled=True
        ).astype(jnp.float32),
        lax.psum_scatter(
            totals[10].astype(jnp.bfloat16), "dp", scatter_dimension=1, tiled=True
        ).astype(jnp.float32),
    )
    whole = (
        lax.all_gather(share_list[0].astype(jnp.bfloat16), "dp", axis=0, tiled=True).astype(
            jnp.float32
        ),
        lax.all_gather(share_list[1].astype(jnp.bfloat16), "dp", axis=1, tiled=True).astype(
            jnp.float32
        ),
        lax.all_gather(share_list[2].astype(jnp.bfloat16), "dp", axis=0, tiled=True).astype(
            jnp.float32
        ),
        lax.all_gather(share_list[3].astype(jnp.bfloat16), "dp", axis=1, tiled=True).astype(
            jnp.float32
        ),
    )
    small = lax.psum(
        (totals[0], totals[1], totals[3], totals[5], totals[6], totals[7], totals[9], totals[11]),
        "dp",
    )
    forward_rows = jnp.stack(results[1:])
    backward_rows = jnp.stack(sent_grads[1:])
    section_out = jnp.where(is_first, backward_rows, forward_rows)[None]
    return (
        section_out,
        small[0][None],
        small[1][None],
        whole[0].reshape(model_width, 3, -1)[None],
        small[2][None],
        whole[1][None],
        small[3][None],
        small[4][None],
        small[5][None],
        whole[2][None],
        small[6][None],
        whole[3][None],
        small[7][None],
    )


def solution(mesh):
    placed = (
        P("pipe", "dp", None, None),
        P("pipe", None),
        P("pipe", None),
        P("pipe", None, None, "mp"),
        P("pipe", None, "mp"),
        P("pipe", "mp", None),
        P("pipe", None),
        P("pipe", None),
        P("pipe", None),
        P("pipe", None, "mp"),
        P("pipe", "mp"),
        P("pipe", "mp", None),
        P("pipe", None),
    )
    return jax.shard_map(
        on_device,
        mesh=mesh,
        in_specs=placed,
        out_specs=(
            P("pipe", "dp", None, None),
            P("pipe", None),
            P("pipe", None),
            P("pipe", None, None, "mp"),
            P("pipe", None, "mp"),
            P("pipe", "mp", None),
            P("pipe", None),
            P("pipe", None),
            P("pipe", None),
            P("pipe", None, "mp"),
            P("pipe", "mp"),
            P("pipe", "mp", None),
            P("pipe", None),
        ),
        check_vma=False,
    )
```

profile of v0, /device:TPU:0, one launch (start us, length us, event | category | flops | bytes accessed | tf_op | source)
XLA Modules:
  0.0 1629.2 jit_solution(3938570287198335092)
XLA Ops:
  27.6 47.4 %all-reduce.18.cloned.1.call-done = bf16[729,1152]{1,0:T(8,128)(2,1)} async-done(((bf16[729,1152]{1,0:T(8,128)(2,1)}), bf16[729,1152]{1,0:T(8,128)(2,1)}) %all-reduce.18.cloned.1.call-update) | async-done | bytes 1679632 | tf_op jit(solution)/shard_map/psum | solution.py:150
  80.3 13.7 convolution_convert_fusion.15
  94.1 45.0 %all-reduce.20.cloned.1.call-done = bf16[729,1152]{1,0:T(8,128)(2,1)} async-done(((bf16[729,1152]{1,0:T(8,128)(2,1)}), bf16[729,1152]{1,0:T(8,128)(2,1)}) %all-reduce.20.cloned.1.call-update) | async-done | bytes 1679632 | tf_op jit(solution)/shard_map/psum | solution.py:160
  148.7 34.8 %collective-permute-done = bf16[729,1152]{1,0:T(8,128)(2,1)} collective-permute-done((bf16[729,1152]{1,0:T(8,128)(2,1)}, bf16[729,1152]{1,0:T(8,128)(2,1)}, u32[]{:S(2)}, u32[]{:S(2)}) %collective-permute-start) | collective-permute-done | bytes 1679648 | tf_op jit(solution)/shard_map/ppermute | solution.py:17
  202.0 46.4 %all-reduce.22.cloned.1.call-done = bf16[729,1152]{1,0:T(8,128)(2,1)} async-done(((bf16[729,1152]{1,0:T(8,128)(2,1)}), bf16[729,1152]{1,0:T(8,128)(2,1)}) %all-reduce.22.cloned.1.call-update) | async-done | bytes 1679632 | tf_op jit(solution)/shard_map/psum | solution.py:150
  258.2 7.0 convert_reduce_fusion.23
  270.2 13.9 convolution_convert_fusion.12
  284.2 72.7 %all-reduce.38.cloned.1.call-done = (bf16[729,1152]{1,0:T(8,128)(2,1)}, bf16[729,1152]{1,0:T(8,128)(2,1)}) async-done(((bf16[729,1152]{1,0:T(8,128)(2,1)}, bf16[729,1152]{1,0:T(8,128)(2,1)}), (bf16[729,1152]{1,0:T(8,128)(2,1)}, bf16[729,1152]{1,0:T(8,128)(2,1)})) %all-reduce.38.cloned.1.call-update) | async-done | bytes 3359248 | tf_op jit(solution)/shard_map/psum | solution.py:207
  369.8 30.1 %collective-permute-done.2 = bf16[729,1152]{1,0:T(8,128)(2,1)S(1)} collective-permute-done((bf16[729,1152]{1,0:T(8,128)(2,1)S(1)}, bf16[729,1152]{1,0:T(8,128)(2,1)S(1)}, u32[]{:S(2)}, u32[]{:S(2)}) %collective-permute-start.2) | collective-permute-done | bytes 1679648 | tf_op jit(solution)/shard_map/ppermute | solution.py:17
  413.0 10.2 multiply_convert_fusion.3
  447.0 71.8 %all-reduce.36.cloned.1.call-done = (bf16[729,1152]{1,0:T(8,128)(2,1)}, bf16[729,1152]{1,0:T(8,128)(2,1)}) async-done(((bf16[729,1152]{1,0:T(8,128)(2,1)}, bf16[729,1152]{1,0:T(8,128)(2,1)}), (bf16[729,1152]{1,0:T(8,128)(2,1)}, bf16[729,1152]{1,0:T(8,128)(2,1)})) %all-reduce.36.cloned.1.call-update) | async-done | bytes 3359248 | tf_op jit(solution)/shard_map/psum | solution.py:222
  530.8 36.7 %collective-permute-done.1 = bf16[729,1152]{1,0:T(8,128)(2,1)} collective-permute-done((bf16[729,1152]{1,0:T(8,128)(2,1)}, bf16[729,1152]{1,0:T(8,128)(2,1)}, u32[]{:S(2)}, u32[]{:S(2)}) %collective-permute-start.1) | collective-permute-done | bytes 1679648 | tf_op jit(solution)/shard_map/ppermute | solution.py:17
  567.5 6.9 fusion.440
  576.6 13.7 convolution_convert_fusion.9
  595.0 6.1 convert_reduce_fusion.22
  606.2 71.9 %all-reduce.34.cloned.1.call-done = (bf16[729,1152]{1,0:T(8,128)(2,1)}, bf16[729,1152]{1,0:T(8,128)(2,1)}) async-done(((bf16[729,1152]{1,0:T(8,128)(2,1)}, bf16[729,1152]{1,0:T(8,128)(2,1)}), (bf16[729,1152]{1,0:T(8,128)(2,1)}, bf16[729,1152]{1,0:T(8,128)(2,1)})) %all-reduce.34.cloned.1.call-update) | async-done | bytes 3359248 | tf_op jit(solution)/shard_map/psum | solution.py:207
  691.5 29.9 %collective-permute-done.4 = bf16[729,1152]{1,0:T(8,128)(2,1)S(1)} collective-permute-done((bf16[729,1152]{1,0:T(8,128)(2,1)S(1)}, bf16[729,1152]{1,0:T(8,128)(2,1)S(1)}, u32[]{:S(2)}, u32[]{:S(2)}) %collective-permute-start.4) | collective-permute-done | bytes 1679648 | tf_op jit(solution)/shard_map/ppermute | solution.py:17
  747.6 10.2 multiply_convert_fusion.2
  763.4 6.7 broadcast_select_fusion.11
  788.2 62.6 %all-reduce.32.cloned.1.call-done = (bf16[729,1152]{1,0:T(8,128)(2,1)}, bf16[729,1152]{1,0:T(8,128)(2,1)}) async-done(((bf16[729,1152]{1,0:T(8,128)(2,1)}, bf16[729,1152]{1,0:T(8,128)(2,1)}), (bf16[729,1152]{1,0:T(8,128)(2,1)}, bf16[729,1152]{1,0:T(8,128)(2,1)})) %all-reduce.32.cloned.1.call-update) | async-done | bytes 3359248 | tf_op jit(solution)/shard_map/psum | solution.py:222
  866.2 32.5 %collective-permute-done.3 = bf16[729,1152]{1,0:T(8,128)(2,1)S(1)} collective-permute-done((bf16[729,1152]{1,0:T(8,128)(2,1)S(1)}, bf16[729,1152]{1,0:T(8,128)(2,1)S(1)}, u32[]{:S(2)}, u32[]{:S(2)}) %collective-permute-start.3) | collective-permute-done | bytes 1679648 | tf_op jit(solution)/shard_map/ppermute | solution.py:17
  901.4 5.6 convert_reduce_fusion.21
  912.4 6.2 fusion.453
  922.9 33.5 %all-reduce.24.cloned.1.call-done = bf16[729,1152]{1,0:T(8,128)(2,1)} async-done(((bf16[729,1152]{1,0:T(8,128)(2,1)}), bf16[729,1152]{1,0:T(8,128)(2,1)}) %all-reduce.24.cloned.1.call-update) | async-done | bytes 1679632 | tf_op jit(solution)/shard_map/psum | solution.py:207
  967.1 6.6 convert_reduce_fusion.26
  978.5 10.2 multiply_convert_fusion.1
  1000.7 42.8 %all-reduce.26.cloned.1.call-done = bf16[729,1152]{1,0:T(8,128)(2,1)} async-done(((bf16[729,1152]{1,0:T(8,128)(2,1)}), bf16[729,1152]{1,0:T(8,128)(2,1)}) %all-reduce.26.cloned.1.call-update) | async-done | bytes 1679632 | tf_op jit(solution)/shard_map/psum | solution.py:222
  1056.3 34.5 %collective-permute-done.5 = bf16[729,1152]{1,0:T(8,128)(2,1)S(1)} collective-permute-done((bf16[729,1152]{1,0:T(8,128)(2,1)S(1)}, bf16[729,1152]{1,0:T(8,128)(2,1)S(1)}, u32[]{:S(2)}, u32[]{:S(2)}) %collective-permute-start.5) | collective-permute-done | bytes 1679648 | tf_op jit(solution)/shard_map/ppermute | solution.py:17
  1105.4 6.2 fusion.235
  1111.6 35.5 %all-reduce.28.cloned.1.call-done = bf16[729,1152]{1,0:T(8,128)(2,1)} async-done(((bf16[729,1152]{1,0:T(8,128)(2,1)}), bf16[729,1152]{1,0:T(8,128)(2,1)}) %all-reduce.28.cloned.1.call-update) | async-done | bytes 1679632 | tf_op jit(solution)/shard_map/psum | solution.py:207
  1156.7 5.4 convert_reduce_fusion.24
  1167.0 10.2 multiply_convert_fusion
  1202.9 6.5 fusion.5
  1209.7 7.9 fusion.432
  1224.7 13.9 convolution_convert_fusion.4
  1238.6 7.9 fusion.433
  1250.7 8.8 fusion.1
  1265.0 24.7 %reduce-scatter.11.cloned.1.call-done = bf16[1076,288]{0,1:T(8,128)(2,1)} async-done(((bf16[1076,1152]{0,1:T(8,128)(2,1)}), bf16[1076,288]{0,1:T(8,128)(2,1)}) %reduce-scatter.11.cloned.1.call-update) | async-done | bytes 619792 | tf_op jit(solution)/shard_map/reduce_scatter | solution.py:330
  1290.8 25.6 %reduce-scatter.15.cloned.1.call-done = bf16[288,288]{1,0:T(8,128)(2,1)} async-done(((bf16[1152,288]{1,0:T(8,128)(2,1)}), bf16[288,288]{1,0:T(8,128)(2,1)}) %reduce-scatter.15.cloned.1.call-update) | async-done | bytes 165904
  1316.4 18.8 %all_gather.13 = bf16[288,1152]{0,1:T(8,128)(2,1)S(1)} all-gather(bf16[288,288]{0,1:T(8,128)(2,1)} %bitcast.466), channel_id=1, replica_groups=mesh['pipe'=2,'dp'=4,'mp'=4] {'dp'}, dimensions={1}, use_global_device_ids=true | all-gather | bytes 829440 | tf_op jit(solution)/shard_map/all_gather | solution.py:338
  1339.7 51.4 %all-reduce.30.cloned.1.call-done = (bf16[729,1152]{1,0:T(8,128)(2,1)}, bf16[729,1152]{1,0:T(8,128)(2,1)}) async-done(((bf16[729,1152]{1,0:T(8,128)(2,1)}, bf16[729,1152]{1,0:T(8,128)(2,1)}), (bf16[729,1152]{1,0:T(8,128)(2,1)}, bf16[729,1152]{1,0:T(8,128)(2,1)})) %all-reduce.30.cloned.1.call-update) | async-done | bytes 3359248 | tf_op jit(solution)/shard_map/psum | solution.py:222
  1394.7 22.3 %all-reduce = (f32[1,1152]{1,0:T(1,128)}, f32[1,1152]{1,0:T(1,128)}, f32[1,2,288]{2,1,0:T(2,128)}, f32[1,1152]{1,0:T(1,128)}, f32[1,1152]{1,0:T(1,128)}, /*index...) all-reduce(f32[1,1152]{1,0:T(1,128)S(1)} %broadcast_in_dim.101, ...), channel_id=1, replica_groups=mesh['pipe'=2,'dp'=4,'mp'=4] {'dp'}, use_global_device_ids=true, to_apply=%region_80.81 | all-reduce | flops 8564 | bytes 68512 | tf_op jit(solution)/shard_map/psum | solution.py:348
  1421.5 26.0 %reduce-scatter.9.cloned.1.call-done = bf16[288,1076]{1,0:T(8,128)(2,1)} async-done(((bf16[1152,1076]{1,0:T(8,128)(2,1)}), bf16[288,1076]{1,0:T(8,128)(2,1)}) %reduce-scatter.9.cloned.1.call-update) | async-done | bytes 619792 | tf_op jit(solution)/shard_map/reduce_scatter | solution.py:327
  1456.2 37.6 %all-gather.4.cloned.1.call-done = bf16[1152,864]{1,0:T(8,128)(2,1)} async-done(((bf16[288,864]{1,0:T(8,128)(2,1)}), bf16[1152,864]{1,0:T(8,128)(2,1)}) %all-gather.4.cloned.1.call-update) | async-done | bytes 1990672 | tf_op jit(solution)/shard_map/all_gather | solution.py:335
  1501.6 47.7 %all-gather.8.cloned.1.call-done = bf16[1076,1152]{0,1:T(8,128)(2,1)} async-done(((bf16[1076,288]{0,1:T(8,128)(2,1)}), bf16[1076,1152]{0,1:T(8,128)(2,1)}) %all-gather.8.cloned.1.call-update) | async-done | bytes 2479120 | tf_op jit(solution)/shard_map/all_gather | solution.py:344
  1553.8 12.8 copy.131
  1566.5 38.3 %all-gather.6.cloned.1.call-done = bf16[1152,1076]{1,0:T(8,128)(2,1)} async-done(((bf16[288,1076]{1,0:T(8,128)(2,1)}), bf16[1152,1076]{1,0:T(8,128)(2,1)}) %all-gather.6.cloned.1.call-update) | async-done | bytes 2479120 | tf_op jit(solution)/shard_map/all_gather | solution.py:341
  1609.3 12.7 copy.130
  (632 shorter events, 381.8 us)
Async XLA Ops:
  7.2 73.1 %copy-start = (bf16[1,1152,1076]{1,2,0:T(8,128)(2,1)S(1)}, bf16[1,1152,1076]{1,2,0:T(8,128)(2,1)}, u32[]{:S(2)}) copy-start(bf16[1,1152,1076]{1,2,0:T(8,128)(2,1)} %param.22) | copy-start | bytes 7437316
  7.2 67.8 %all-reduce.18.cloned.1.call-start = ((), (), s32[]{:S(2)}) async-start(), calls=%async_computation.4 | async-start | bytes 3391488 | tf_op jit(solution)/shard_map/psum | solution.py:150
  27.2 111.9 %all-reduce.20.cloned.1.call-start = ((), (), s32[]{:S(2)}) async-start(), calls=%async_computation.5 | async-start | bytes 3391488 | tf_op jit(solution)/shard_map/psum | solution.py:160
  94.0 154.4 %all-reduce.22.cloned.1.call-start = ((), (), s32[]{:S(2)}) async-start(), calls=%async_computation.6 | async-start | bytes 3391488 | tf_op jit(solution)/shard_map/psum | solution.py:150
  94.1 584.1 %copy-start.108 = (f32[1152]{0:T(1024)}, f32[1152]{0:T(1024)S(1)}, u32[]{:S(2)}) copy-start(f32[1152]{0:T(1024)S(1)} %convert_reduce_fusion.32) | copy-start | bytes 13828
  143.7 39.8 %collective-permute-start = (bf16[729,1152]{1,0:T(8,128)(2,1)}, bf16[729,1152]{1,0:T(8,128)(2,1)}, u32[]{:S(2)}, u32[]{:S(2)}) collective-permute-start(bf16[729,1152]{1,0:T(8,128)(2,1)} %add_convert_fusion.10), channel_id=1, source_target_pairs={{0,16},{1,17},{2,18},{3,19},{4,20},{5,21},{6,22},{7,23},{8,24},{9,... | collective-permute-start | bytes 5038856 | tf_op jit(solution)/shard_map/ppermute | solution.py:17
  201.7 155.2 %all-reduce.38.cloned.1.call-start = ((), (), s32[]{:S(2)}) async-start(), calls=%async_computation.21 | async-start | bytes 6782976 | tf_op jit(solution)/shard_map/psum | solution.py:207
  255.0 144.8 %copy-start.110 = (f32[729]{0:T(1024)}, f32[729]{0:T(1024)S(1)}, u32[]{:S(2)}) copy-start(f32[729]{0:T(1024)S(1)} %broadcast_multiply_fusion.28) | copy-start | bytes 8752
  255.5 144.3 %copy-start.116 = (f32[729]{0:T(1024)}, f32[729]{0:T(1024)S(1)}, u32[]{:S(2)}) copy-start(f32[729]{0:T(1024)S(1)} %add_rsqrt_fusion.12) | copy-start | bytes 8752
  284.2 234.6 %all-reduce.36.cloned.1.call-start = ((), (), s32[]{:S(2)}) async-start(), calls=%async_computation.20 | async-start | bytes 6782976 | tf_op jit(solution)/shard_map/psum | solution.py:222
  360.4 39.5 %collective-permute-start.2 = (bf16[729,1152]{1,0:T(8,128)(2,1)S(1)}, bf16[729,1152]{1,0:T(8,128)(2,1)S(1)}, u32[]{:S(2)}, u32[]{:S(2)}) collective-permute-start(bf16[729,1152]{1,0:T(8,128)(2,1)S(1)} %add_convert_fusion.7), channel_id=1, source_target_pairs={{0,16},{1,17},{2,18},{3,19},{4,20},{5,21},{6,22},{7,23},{8,24},{9,... | collective-permute-start | bytes 5038856 | tf_op jit(solution)/shard_map/ppermute | solution.py:17
  364.4 35.4 %slice-start = ((s8[5087232]{0:T(1024)(128)(4,1)}), s8[4194304]{0:T(1024)(128)(4,1)S(1)}, s32[]{:S(2)}) async-start(s8[5087232]{0:T(1024)(128)(4,1)} %bitcast.390), calls=%async_computation.22 | async-start | bytes 8388608
  364.5 35.4 %slice-start.1 = ((s8[5087232]{0:T(1024)(128)(4,1)}), s8[892928]{0:T(1024)(128)(4,1)S(1)}, s32[]{:S(2)}) async-start(s8[5087232]{0:T(1024)(128)(4,1)} %bitcast.390), calls=%async_computation.23 | async-start | bytes 1785856
  365.9 42.3 %copy-start.1 = (f32[4,729,729]{1,2,0:T(8,128)}, f32[4,729,729]{1,2,0:T(8,128)S(1)}, u32[]{:S(2)}) copy-start(f32[4,729,729]{1,2,0:T(8,128)S(1)} %fusion.450) | copy-start | bytes 25509172
  444.8 233.3 %all-reduce.34.cloned.1.call-start = ((), (), s32[]{:S(2)}) async-start(), calls=%async_computation.19 | async-start | bytes 6782976 | tf_op jit(solution)/shard_map/psum | solution.py:207
  444.9 81.9 %copy-start.114 = (f32[729]{0:T(1024)}, f32[729]{0:T(1024)S(1)}, u32[]{:S(2)}) copy-start(f32[729]{0:T(1024)S(1)} %broadcast_multiply_fusion.25) | copy-start | bytes 8752
  446.9 79.8 %copy-start.120 = (f32[729]{0:T(1024)}, f32[729]{0:T(1024)S(1)}, u32[]{:S(2)}) copy-start(f32[729]{0:T(1024)S(1)} %add_rsqrt_fusion.11) | copy-start | bytes 8752
  526.7 40.8 %collective-permute-start.1 = (bf16[729,1152]{1,0:T(8,128)(2,1)}, bf16[729,1152]{1,0:T(8,128)(2,1)}, u32[]{:S(2)}, u32[]{:S(2)}) collective-permute-start(bf16[729,1152]{1,0:T(8,128)(2,1)} %fusion.121), channel_id=1, source_target_pairs={{16,0},{17,1},{18,2},{19,3},{20,4},{21,5},{22,6},{23,7},{24,8},{25... | collective-permute-start | bytes 5038856 | tf_op jit(solution)/shard_map/ppermute | solution.py:17
  528.0 39.5 %copy-start.4 = (bf16[729,1152]{1,0:T(8,128)(2,1)S(1)}, bf16[729,1152]{1,0:T(8,128)(2,1)}, u32[]{:S(2)}) copy-start(bf16[729,1152]{1,0:T(8,128)(2,1)} %get-tuple-element.155) | copy-start | bytes 5038852
  528.1 39.5 %copy-start.39 = (bf16[729,1152]{1,0:T(8,128)(2,1)S(1)}, bf16[729,1152]{1,0:T(8,128)(2,1)}, u32[]{:S(2)}) copy-start(bf16[729,1152]{1,0:T(8,128)(2,1)} %all-reduce.18.cloned.1.call-done) | copy-start | bytes 5038852
  574.4 113.1 %copy-start.112 = (f32[729]{0:T(1024)}, f32[729]{0:T(1024)S(1)}, u32[]{:S(2)}) copy-start(f32[729]{0:T(1024)S(1)} %broadcast_multiply_fusion.20) | copy-start | bytes 8752
  576.6 110.9 %copy-start.118 = (f32[729]{0:T(1024)}, f32[729]{0:T(1024)S(1)}, u32[]{:S(2)}) copy-start(f32[729]{0:T(1024)S(1)} %add_rsqrt_fusion.8) | copy-start | bytes 8752
  606.2 244.7 %all-reduce.32.cloned.1.call-start = ((), (), s32[]{:S(2)}) async-start(), calls=%async_computation.18 | async-start | bytes 6782976 | tf_op jit(solution)/shard_map/psum | solution.py:222
  681.7 39.7 %collective-permute-start.4 = (bf16[729,1152]{1,0:T(8,128)(2,1)S(1)}, bf16[729,1152]{1,0:T(8,128)(2,1)S(1)}, u32[]{:S(2)}, u32[]{:S(2)}) collective-permute-start(bf16[729,1152]{1,0:T(8,128)(2,1)S(1)} %add_convert_fusion.4), channel_id=1, source_target_pairs={{0,16},{1,17},{2,18},{3,19},{4,20},{5,21},{6,22},{7,23},{8,24},{9,... | collective-permute-start | bytes 5038856 | tf_op jit(solution)/shard_map/ppermute | solution.py:17
  689.8 31.6 %copy-start.5 = (bf16[729,1152]{1,0:T(8,128)(2,1)S(1)}, bf16[729,1152]{1,0:T(8,128)(2,1)}, u32[]{:S(2)}) copy-start(bf16[729,1152]{1,0:T(8,128)(2,1)} %get-tuple-element.155) | copy-start | bytes 5038852
  777.0 179.5 %all-reduce.24.cloned.1.call-start = ((), (), s32[]{:S(2)}) async-start(), calls=%async_computation.7 | async-start | bytes 3391488 | tf_op jit(solution)/shard_map/psum | solution.py:207
  858.2 40.6 %collective-permute-start.3 = (bf16[729,1152]{1,0:T(8,128)(2,1)S(1)}, bf16[729,1152]{1,0:T(8,128)(2,1)S(1)}, u32[]{:S(2)}, u32[]{:S(2)}) collective-permute-start(bf16[729,1152]{1,0:T(8,128)(2,1)S(1)} %fusion.114), channel_id=1, source_target_pairs={{16,0},{17,1},{18,2},{19,3},{20,4},{21,5},{22,6},{23,7},{24,8},{25... | collective-permute-start | bytes 5038856 | tf_op jit(solution)/shard_map/ppermute | solution.py:17
  866.2 40.8 %copy-start.172 = (f32[729,1076]{0,1:T(8,128)}, f32[729,1076]{0,1:T(8,128)S(1)}, u32[]{:S(2)}) copy-start(f32[729,1076]{0,1:T(8,128)S(1)} %convolution_add_fusion.3) | copy-start | bytes 9412852
  866.2 35.1 %copy-start.153 = (bf16[1,1076,1152]{2,1,0:T(8,128)(2,1)S(1)}, bf16[1,1076,1152]{2,1,0:T(8,128)(2,1)}, u32[]{:S(2)}) copy-start(bf16[1,1076,1152]{2,1,0:T(8,128)(2,1)} %param.24) | copy-start | bytes 7437316
  912.1 131.3 %all-reduce.26.cloned.1.call-start = ((), (), s32[]{:S(2)}) async-start(), calls=%async_computation.8 | async-start | bytes 3391488 | tf_op jit(solution)/shard_map/psum | solution.py:222
  998.3 148.8 %all-reduce.28.cloned.1.call-start = ((), (), s32[]{:S(2)}) async-start(), calls=%async_computation.9 | async-start | bytes 3391488 | tf_op jit(solution)/shard_map/psum | solution.py:207
  1050.2 40.7 %collective-permute-start.5 = (bf16[729,1152]{1,0:T(8,128)(2,1)S(1)}, bf16[729,1152]{1,0:T(8,128)(2,1)S(1)}, u32[]{:S(2)}, u32[]{:S(2)}) collective-permute-start(bf16[729,1152]{1,0:T(8,128)(2,1)S(1)} %fusion.107), channel_id=1, source_target_pairs={{16,0},{17,1},{18,2},{19,3},{20,4},{21,5},{22,6},{23,7},{24,8},{25... | collective-permute-start | bytes 5038856 | tf_op jit(solution)/shard_map/ppermute | solution.py:17
  1056.3 41.6 %copy-start.175 = (f32[729,1076]{0,1:T(8,128)}, f32[729,1076]{0,1:T(8,128)S(1)}, u32[]{:S(2)}) copy-start(f32[729,1076]{0,1:T(8,128)S(1)} %convolution_add_fusion.2) | copy-start | bytes 9412852
  1056.3 36.6 %copy-start.154 = (bf16[1,1076,1152]{2,1,0:T(8,128)(2,1)S(1)}, bf16[1,1076,1152]{2,1,0:T(8,128)(2,1)}, u32[]{:S(2)}) copy-start(bf16[1,1076,1152]{2,1,0:T(8,128)(2,1)} %param.24) | copy-start | bytes 7437316
  1102.9 161.5 %reduce-scatter.13.cloned.1.call-start = ((), (), s32[]{:S(2)}) async-start(), calls=%async_computation.15 | async-start | bytes 2580480 | tf_op jit(solution)/shard_map/reduce_scatter | solution.py:321
  1191.7 98.0 %reduce-scatter.11.cloned.1.call-start = ((), (), s32[]{:S(2)}) async-start(), calls=%async_computation.13 | async-start | bytes 3317760 | tf_op jit(solution)/shard_map/reduce_scatter | solution.py:330
  1209.4 106.9 %reduce-scatter.15.cloned.1.call-start = ((), (), s32[]{:S(2)}) async-start(), calls=%async_computation.16 | async-start | bytes 1105920
  1224.7 166.3 %all-reduce.30.cloned.1.call-start = ((), (), s32[]{:S(2)}) async-start(), calls=%async_computation.17 | async-start | bytes 6782976 | tf_op jit(solution)/shard_map/psum | solution.py:222
  1250.0 197.4 %reduce-scatter.9.cloned.1.call-start = ((), (), s32[]{:S(2)}) async-start(), calls=%async_computation.11 | async-start | bytes 3317760 | tf_op jit(solution)/shard_map/reduce_scatter | solution.py:327
  1264.3 26.2 %copy-start.123 = (f32[1152]{0:T(1024)S(1)}, f32[1152]{0:T(1024)}, u32[]{:S(2)}) copy-start(f32[1152]{0:T(1024)} %get-tuple-element.165) | copy-start | bytes 13828
  1264.3 229.5 %all-gather.4.cloned.1.call-start = ((), (), s32[]{:S(2)}) async-start(), calls=%async_computation.10 | async-start | bytes 2580480 | tf_op jit(solution)/shard_map/all_gather | solution.py:335
  1264.9 284.4 %all-gather.8.cloned.1.call-start = ((), (), s32[]{:S(2)}) async-start(), calls=%async_computation.14 | async-start | bytes 3317760 | tf_op jit(solution)/shard_map/all_gather | solution.py:344
  1289.7 315.1 %all-gather.6.cloned.1.call-start = ((), (), s32[]{:S(2)}) async-start(), calls=%async_computation.12 | async-start | bytes 3317760 | tf_op jit(solution)/shard_map/all_gather | solution.py:341
  1336.5 58.1 %copy-start.130 = (f32[1152]{0:T(1024)S(1)}, f32[1152]{0:T(1024)}, u32[]{:S(2)}) copy-start(f32[1152]{0:T(1024)} %get-tuple-element.88) | copy-start | bytes 13828
  1336.5 58.1 %copy-start.131 = (f32[1152]{0:T(1024)S(1)}, f32[1152]{0:T(1024)}, u32[]{:S(2)}) copy-start(f32[1152]{0:T(1024)} %get-tuple-element.108) | copy-start | bytes 13828
  1336.5 58.1 %copy-start.134 = (f32[1152]{0:T(1024)S(1)}, f32[1152]{0:T(1024)}, u32[]{:S(2)}) copy-start(f32[1152]{0:T(1024)} %get-tuple-element.90) | copy-start | bytes 13828
  1336.5 58.1 %copy-start.135 = (f32[1152]{0:T(1024)S(1)}, f32[1152]{0:T(1024)}, u32[]{:S(2)}) copy-start(f32[1152]{0:T(1024)} %get-tuple-element.109) | copy-start | bytes 13828
  1336.5 80.5 %copy-start.109 = (f32[1152]{0:T(1024)S(1)}, f32[1152]{0:T(1024)}, u32[]{:S(2)}) copy-start(f32[1152]{0:T(1024)} %copy-done.108) | copy-start | bytes 13828
  (163 other events, 1082.5 us)
Sparse Core Ops, SparseCore 0:
  27.3 47.6 all-reduce.17
  94.1 44.9 all-reduce.19
  201.9 46.4 all-reduce.21
  284.3 72.6 all-reduce.37
  444.9 73.7 all-reduce.35
  606.3 71.8 all-reduce.33
  777.1 73.7 all-reduce.31
  912.2 44.1 all-reduce.23
  998.5 44.9 all-reduce.25
  1103.1 44.0 all-reduce.27
  1191.8 43.1 reduce-scatter.12
  1237.7 51.9 reduce-scatter.10
  1292.0 24.2 reduce-scatter.14
  1319.3 71.6 all-reduce.29
  1393.7 53.6 reduce-scatter.8
  1448.9 44.8 all-gather.3
  1495.2 54.0 all-gather.7
  1550.8 54.0 all-gather.5
where the time goes:
time: 1640 us; the launch traced here: 1630 us
  waiting for transfers between devices  980 us (60%)
  matrix products  304 us (19%)
  other arithmetic  195 us (12%)
  local copies, waits for them, and re-layouts  72 us (4%)
  blocking collectives  41.1 us (3%)
  starting transfers between devices  19.7 us (1%)
  between operations  17.4 us (1%)
    psum x4, waiting for transfers between devices, layer_backward(): lax.psum(jnp.einsum('sc,dc->sd', d_packed, w_qkv, preferred_element_type=...  229 us
    psum x4, waiting for transfers between devices, layer_backward(): lax.psum(jnp.einsum('sf,df->sd', d_pre, w_fc1, preferred_element_type=jnp...  214 us
    ppermute x6, waiting for transfers between devices, shifted(): return lax.ppermute(value, axis, pairs)  199 us
    psum x2, waiting for transfers between devices, layer_forward(): lax.psum(jnp.dot(mixed_low, w_out, preferred_element_type=jnp.float32).as...  93.8 us
    unnamed x378, local copies, waits for them, and re-layouts  62.6 us
    dot_general x4, matrix products, layer_forward(): jnp.dot(act_out.astype(jnp.bfloat16), w_fc2, preferred_element_type=jnp.f...  55.3 us
    all_gather x1, waiting for transfers between devices, on_device(): lax.all_gather(share_list[3].astype(jnp.bfloat16), 'dp', axis=1, tiled=True)  47.7 us
    psum x1, waiting for transfers between devices, layer_forward(): lax.psum(jnp.dot(act_out.astype(jnp.bfloat16), w_fc2, preferred_element_t...  45 us
  transfers between devices with their start and end apart: 24, of which 23 were waited for; matrix products, arithmetic and copies ran while one was open for 10% of the time, Pallas kernels for 0%

commit v1 on v0

v1 whole, which is shorter than its diff:
```python
import functools

import jax
import jax.numpy as jnp
from jax import lax
from jax.experimental import pallas as pl
from jax.experimental.pallas import tpu as pltpu
from jax.sharding import PartitionSpec as P

HDIM = 72
HPAD = 128
EPSILON = 1e-06
GELU_SCALE = 0.7978845608028654
GELU_CUBIC = 0.044715
MESH = pl.DeviceIdType.MESH
BF = jnp.bfloat16
F32 = jnp.float32
CHUNK = 256
HALF = CHUNK // 2
VMEM_LIMIT = 67043328


def dot_nn(a, b):
    return lax.dot_general(a, b, (((1,), (0,)), ((), ())), preferred_element_type=F32)


def dot_nt(a, b):
    return lax.dot_general(a, b, (((1,), (1,)), ((), ())), preferred_element_type=F32)


def dot_tn(a, b):
    return lax.dot_general(a, b, (((0,), (0,)), ((), ())), preferred_element_type=F32)


def col_sum(v):
    return jnp.sum(v, axis=0, keepdims=True)


def norm_stats(v):
    center = v - jnp.mean(v, axis=-1, keepdims=True)
    inv = lax.rsqrt(jnp.mean(center * center, axis=-1, keepdims=True) + EPSILON)
    return center * inv, inv


def norm_back(e, hat, inv, gain):
    d_hat = e * gain
    mean_d = jnp.mean(d_hat, axis=-1, keepdims=True)
    mean_dx = jnp.mean(d_hat * hat, axis=-1, keepdims=True)
    return inv * (d_hat - mean_d - hat * mean_dx)


class Spot:
    def __init__(self, rows):
        self.stage = lax.axis_index("pipe")
        me = lax.axis_index("mp")
        self.rows = rows
        self.core = lax.rem(me, 2)
        self.row = lax.div(me, 2)
        self.sib = self.row * 2 + (1 - self.core)
        self.piece = HALF // rows

    def ahead(self, j):
        return lax.rem(self.row + j, self.rows)

    def behind(self, j):
        return lax.rem(self.row + self.rows - j, self.rows)

    def peer(self, row):
        return {"mp": row * 2 + self.core}


def enter(spot):
    barrier = pltpu.get_barrier_semaphore()
    targets = [{"mp": spot.sib}, {"pipe": 1 - spot.stage}]
    targets += [spot.peer(spot.ahead(j)) for j in range(1, spot.rows)]
    for target in targets:
        pl.semaphore_signal(barrier, inc=1, device_id=target, device_id_type=MESH)
    pl.semaphore_wait(barrier, len(targets))


def remote(src, dst, send, recv, target):
    return pltpu.make_async_remote_copy(
        src_ref=src, dst_ref=dst, send_sem=send, recv_sem=recv, device_id=target, device_id_type=MESH
    )


class Gather:
    def __init__(self, buf, ssem, rsem, kind, spot):
        self.buf, self.ssem, self.rsem, self.kind, self.spot = buf, ssem, rsem, kind, spot

    def view(self, c, row):
        p = self.spot.piece
        start = c * CHUNK + self.spot.core * HALF + row * p
        return self.buf.at[pl.ds(pl.multiple_of(start, p), p)]

    def mine(self, c):
        return self.view(c, self.spot.row)

    def copy(self, c, which, view, target):
        k = self.kind + which
        return remote(view, view, self.ssem.at[k, c], self.rsem.at[k, c], target)

    def near_copy(self, c):
        return self.copy(c, 0, self.mine(c), {"mp": self.spot.sib})

    def far_copy(self, c, j):
        return self.copy(c, 2 * j - 1, self.mine(c), self.spot.peer(self.spot.ahead(j)))

    def pass_copy(self, c, j):
        return self.copy(c, 2 * j, self.view(c, self.spot.behind(j)), {"mp": self.spot.sib})

    def start(self, c):
        for j in range(1, self.spot.rows):
            self.far_copy(c, j).start()
        self.near_copy(c).start()

    def forward(self, c):
        for j in range(1, self.spot.rows):
            self.far_copy(c, j).wait_recv()
            self.pass_copy(c, j).start()

    def finish(self, c):
        self.near_copy(c).wait_recv()
        for j in range(1, self.spot.rows):
            self.pass_copy(c, j).wait_recv()

    def drain(self, c):
        self.near_copy(c).wait_send()
        for j in range(1, self.spot.rows):
            self.far_copy(c, j).wait_send()
            self.pass_copy(c, j).wait_send()


class Reduce:
    def __init__(self, part, near, out, far, ssem, rsem, kind, spot):
        self.part, self.near, self.out, self.far = part, near, out, far
        self.ssem, self.rsem, self.kind, self.spot = ssem, rsem, kind, spot

    def near_copy(self, c):
        src = self.part.at[c, pl.ds(pl.multiple_of((1 - self.spot.core) * HALF, HALF), HALF)]
        k = self.kind
        return remote(src, self.near.at[c], self.ssem.at[k, c], self.rsem.at[k, c], {"mp": self.spot.sib})

    def far_copy(self, c, j):
        k = self.kind + j
        target = self.spot.peer(self.spot.ahead(j))
        return remote(
            self.out.at[c, j - 1], self.far.at[c, j - 1], self.ssem.at[k, c], self.rsem.at[k, c], target
        )

    def start(self, c, value):
        self.part[c] = value.astype(BF)
        self.near_copy(c).start()

    def pair(self, c, row):
        p = self.spot.piece
        own = self.part[c, pl.ds(pl.multiple_of(self.spot.core * HALF + row * p, p), p)]
        near = self.near[c, pl.ds(pl.multiple_of(row * p, p), p)]
        return own.astype(F32) + near.astype(F32)

    def cross(self, c):
        self.near_copy(c).wait_recv()
        for j in range(1, self.spot.rows):
            self.out[c, j - 1] = self.pair(c, self.spot.ahead(j)).astype(BF)
            self.far_copy(c, j).start()

    def result(self, c):
        total = self.pair(c, self.spot.row)
        for j in range(1, self.spot.rows):
            self.far_copy(c, j).wait_recv()
            total = total + self.far[c, j - 1].astype(F32)
        return total

    def drain(self, c):
        self.near_copy(c).wait_send()
        for j in range(1, self.spot.rows):
            self.far_copy(c, j).wait_send()


def forward_kernel(
    images, chunks, heads, length, scaling, rows_mp,
    x_hbm, vec, bqkv, wqkv, wout, w1, w2,
    y_o, xin_o, a1_o, qkv_o, o_o, lse_o, a2_o, g_o, sl_o, h1_o,
    xbuf, a1b, qkvb, ob, lseb, a2b, gb, slb, h1b, outb,
    part1, near1, out1, far1, part2, near2, out2, far2,
    ssem, rsem, psend, precv, lsem,
):
    spot = Spot(rows_mp)
    stage, piece = spot.stage, spot.piece
    hw = heads * HPAD

    load = pltpu.make_async_copy(x_hbm, xbuf, lsem.at[0])

    @pl.when(stage == 0)
    def _():
        load.start()

    enter(spot)
    kinds = sem_kinds(rows_mp)
    gat2 = Gather(a2b, ssem, rsem, kinds[1], spot)
    red1 = Reduce(part1, near1, out1, far1, ssem, rsem, kinds[2], spot)
    red2 = Reduce(part2, near2, out2, far2, ssem, rsem, kinds[3], spot)

    def gat1(i):
        return Gather(a1b.at[lax.rem(i, 2)], ssem, rsem, kinds[0], spot)

    def vrow(r):
        return vec[r : r + 1, :]

    def pipe_copy(i, c):
        return remote(
            outb.at[pl.ds(c * piece, piece)],
            xbuf.at[i, pl.ds(c * piece, piece)],
            psend.at[c],
            precv.at[i, c],
            {"pipe": 1},
        )

    def y_copy(i, c):
        return pltpu.make_async_copy(
            outb.at[pl.ds(c * piece, piece)], y_o.at[i, pl.ds(c * piece, piece)], psend.at[c]
        )

    def begin(i, c):
        @pl.when(stage == 1)
        def _():
            pipe_copy(i, c).wait_recv()

        v = xbuf[i, pl.ds(c * piece, piece)].astype(F32)
        hat, _ = norm_stats(v)
        gat1(i).mine(c)[...] = (hat * vrow(0) + vrow(1)).astype(BF)
        gat1(i).start(c)

    def project(i, c):
        gat1(i).finish(c)
        a = a1b[lax.rem(i, 2), pl.ds(c * CHUNK, CHUNK)]
        qkvb[pl.ds(c * CHUNK, CHUNK)] = (dot_nt(a, wqkv[...]) + bqkv[...]).astype(BF)

    def attend(c):
        rows = pl.ds(c * CHUNK, CHUNK)
        total = chunks * CHUNK
        valid = lax.broadcasted_iota(jnp.int32, (CHUNK, total), 1) < length
        lane = lax.broadcasted_iota(jnp.int32, (CHUNK, HPAD), 1)
        kept = jnp.zeros((CHUNK, HPAD), F32)
        for h in range(heads):
            q = qkvb[rows, h * HPAD : (h + 1) * HPAD]
            k = qkvb[:, hw + h * HPAD : hw + (h + 1) * HPAD]
            v = qkvb[:, 2 * hw + h * HPAD : 2 * hw + (h + 1) * HPAD]
            s = jnp.where(valid, dot_nt(q, k) * scaling, -1e30)
            m = jnp.max(s, axis=-1, keepdims=True)
            e = jnp.exp(s - m)
            t = jnp.sum(e, axis=-1, keepdims=True)
            p = (e / t).astype(BF)
            ob[rows, h * HPAD : (h + 1) * HPAD] = dot_nn(p, v).astype(BF)
            kept = jnp.where(lane == h, m + jnp.log(t), kept)
        lseb[rows] = kept
        red1.start(c, dot_nn(ob[rows], wout[...]))

    def middle(i, c):
        sl = pl.ds(c * piece, piece)
        h1 = xbuf[i, sl].astype(F32) + red1.result(c) + vrow(2)
        h1b[sl] = h1
        hat, _ = norm_stats(h1)
        gat2.mine(c)[...] = (hat * vrow(3) + vrow(4)).astype(BF)
        gat2.start(c)

    def feed(c):
        rows = pl.ds(c * CHUNK, CHUNK)
        gat2.finish(c)
        u = dot_nt(a2b[rows], w1[...]) + vec[5:6, 0 : w1.shape[0]]
        uu = u * u
        t = jnp.tanh(GELU_SCALE * (u + GELU_CUBIC * uu * u))
        half = 0.5 * (1.0 + t)
        gb[rows] = (u * half).astype(BF)
        slb[rows] = (
            half + 0.5 * u * (1.0 - t * t) * (GELU_SCALE * (1.0 + 3.0 * GELU_CUBIC * uu))
        ).astype(BF)
        red2.start(c, dot_nn(gb[rows], w2[...]))

    def end(i, c):
        sl = pl.ds(c * piece, piece)
        outb[sl] = (h1b[sl] + red2.result(c) + vrow(6)).astype(BF)

        @pl.when(stage == 0)
        def _():
            pipe_copy(i, c).start()

        @pl.when(stage == 1)
        def _():
            y_copy(i, c).start()

    def end_wait(i, c):
        @pl.when(stage == 0)
        def _():
            pipe_copy(i, c).wait_send()

        @pl.when(stage == 1)
        def _():
            y_copy(i, c).wait()

    def saves(i):
        return [
            pltpu.make_async_copy(a, b, lsem.at[1 + n])
            for n, (a, b) in enumerate(
                (
                    (a1b.at[lax.rem(i, 2)], a1_o.at[i]),
                    (qkvb, qkv_o.at[i]),
                    (ob, o_o.at[i]),
                    (lseb, lse_o.at[i]),
                    (a2b, a2_o.at[i]),
                    (gb, g_o.at[i]),
                    (slb, sl_o.at[i]),
                    (h1b, h1_o.at[i]),
                    (xbuf.at[i], xin_o.at[i]),
                )
            )
        ]

    @pl.when(stage == 0)
    def _():
        load.wait()

    every = range(chunks)

    def first(i):
        for c in every:
            begin(i, c)

    def second(i):
        for c in every:
            gat1(i).forward(c)
        for c in every:
            project(i, c)
        for c in every:
            gat1(i).drain(c)

    first(0)
    second(0)

    def image(i, carry):
        sv = saves(i)
        sv[0].start()
        sv[1].start()
        for s in range(chunks + 6):
            def at(j):
                return s - j if 0 <= s - j < chunks else None

            c = at(0)
            if c is not None:
                attend(c)
            c = at(1)
            if c is not None:
                red1.cross(c)
            c = at(5)
            if c is not None:
                red2.cross(c)
            c = at(2)
            if c is not None:
                middle(i, c)
            c = at(3)
            if c is not None:
                gat2.forward(c)
            c = at(6)
            if c is not None:
                end(i, c)
            c = at(4)
            if c is not None:
                feed(c)
            if s == chunks:
                sv[2].start()
                sv[3].start()
        for n in range(4, 9):
            sv[n].start()
        for n in range(9):
            sv[n].wait()

        @pl.when(i + 1 < images)
        def _():
            first(i + 1)

        for c in every:
            red1.drain(c)
            red2.drain(c)
            gat2.drain(c)
            end_wait(i, c)

        @pl.when(i + 1 < images)
        def _():
            second(i + 1)

        return carry

    lax.fori_loop(0, images, image, 0)


def backward_kernel(
    images, chunks, heads, length, scaling, rows_mp,
    d_hbm, vec, wqkv, wout, w1, w2,
    xin_i, a1_i, qkv_i, o_i, lse_i, a2_i, g_i, sl_i, h1_i,
    dx_o, gqkv, gout, g1, g2, small, gbqkv,
    dbuf, xinb, a1b, qkvb, ob, lseb, a2b, gb, slb, h1b, dmb, dab, dqb, dkv, dob, outb,
    part1, near1, out1, far1, part2, near2, out2, far2,
    ssem, rsem, psend, precv, lsem,
):
    spot = Spot(rows_mp)
    stage, piece = spot.stage, spot.piece
    hw = heads * HPAD
    load = pltpu.make_async_copy(d_hbm, dbuf, lsem.at[0])

    @pl.when(stage == 1)
    def _():
        load.start()

    def loads(i):
        return [
            pltpu.make_async_copy(b, a, lsem.at[1 + n])
            for n, (a, b) in enumerate(
                (
                    (a1b, a1_i.at[i]),
                    (qkvb, qkv_i.at[i]),
                    (ob, o_i.at[i]),
                    (lseb, lse_i.at[i]),
                    (a2b, a2_i.at[i]),
                    (gb, g_i.at[i]),
                    (slb, sl_i.at[i]),
                    (h1b, h1_i.at[i]),
                    (xinb, xin_i.at[i]),
                )
            )
        ]

    for ld in loads(0):
        ld.start()
    enter(spot)
    kinds = sem_kinds(rows_mp)
    gatm = Gather(dmb, ssem, rsem, kinds[0], spot)
    gata = Gather(dab, ssem, rsem, kinds[1], spot)
    red1 = Reduce(part1, near1, out1, far1, ssem, rsem, kinds[2], spot)
    red2 = Reduce(part2, near2, out2, far2, ssem, rsem, kinds[3], spot)
    every = range(chunks)

    gqkv[...] = jnp.zeros_like(gqkv)
    gout[...] = jnp.zeros_like(gout)
    g1[...] = jnp.zeros_like(g1)
    g2[...] = jnp.zeros_like(g2)
    small[...] = jnp.zeros_like(small)
    gbqkv[...] = jnp.zeros_like(gbqkv)

    def add(r, v):
        small[r : r + 1, :] += v

    def pipe_copy(i, c):
        return remote(
            outb.at[pl.ds(c * piece, piece)],
            dbuf.at[i, pl.ds(c * piece, piece)],
            psend.at[c],
            precv.at[i, c],
            {"pipe": 0},
        )

    def x_copy(i, c):
        return pltpu.make_async_copy(
            outb.at[pl.ds(c * piece, piece)], dx_o.at[i, pl.ds(c * piece, piece)], psend.at[c]
        )

    def begin(i, c):
        @pl.when(stage == 0)
        def _():
            pipe_copy(i, c).wait_recv()

        v = dbuf[i, pl.ds(c * piece, piece)]
        gatm.mine(c)[...] = v
        gatm.start(c)
        add(6, col_sum(v.astype(F32)))

    def feed(c):
        rows = pl.ds(c * CHUNK, CHUNK)
        gatm.finish(c)
        du = (dot_nt(dmb[rows], w2[...]) * slb[rows].astype(F32)).astype(BF)
        slb[rows] = du
        small[5:6, 0 : w1.shape[0]] += col_sum(du.astype(F32))
        red1.start(c, dot_nn(du, w1[...]))

    def middle(i, c):
        sl = pl.ds(c * piece, piece)
        e = red1.result(c)
        hat, inv = norm_stats(h1b[sl])
        add(3, col_sum(e * hat))
        add(4, col_sum(e))
        dh = dbuf[i, sl].astype(F32) + norm_back(e, hat, inv, vec[3:4, :])
        h1b[sl] = dh
        add(2, col_sum(dh))
        gata.mine(c)[...] = dh.astype(BF)
        gata.start(c)

    def weights(acc, a, b, step):
        def tile(n, carry):
            cols = pl.ds(pl.multiple_of(n * step, step), step)
            acc[cols] += dot_tn(a[:, cols], b[...])
            return carry

        lax.fori_loop(0, acc.shape[0] // step, tile, 0)

    def attend(c):
        rows = pl.ds(c * CHUNK, CHUNK)
        total = chunks * CHUNK
        valid = lax.broadcasted_iota(jnp.int32, (CHUNK, total), 1) < length
        gata.finish(c)
        dob[...] = dot_nt(dab[rows], wout[...]).astype(BF)
        for h in range(heads):
            cq = slice(h * HPAD, (h + 1) * HPAD)
            ck = slice(hw + h * HPAD, hw + (h + 1) * HPAD)
            cv = slice(2 * hw + h * HPAD, 2 * hw + (h + 1) * HPAD)
            q, k, v = qkvb[rows, cq], qkvb[:, ck], qkvb[:, cv]
            d = dob[:, cq]
            s = dot_nt(q, k) * scaling
            p = jnp.where(valid, jnp.exp(s - lseb[rows, h : h + 1]), 0.0)
            dv = dot_tn(p.astype(BF), d)
            dp = dot_nt(d, v)
            inner = jnp.sum(dp * p, axis=-1, keepdims=True)
            ds = (p * (dp - inner)).astype(BF)
            dq = (dot_nn(ds, k) * scaling).astype(BF)
            dqb[rows, cq] = dq
            gbqkv[0:1, cq] += col_sum(dq.astype(F32))
            dk = dot_tn(ds, q)
            if c == 0:
                dkv[:, cq] = dk
                dkv[:, ck] = dv
            else:
                dkv[:, cq] += dk
                dkv[:, ck] += dv

    def close():
        dk = (dkv[:, 0:hw] * scaling).astype(BF)
        dqb[:, hw : 2 * hw] = dk
        dv = dkv[:, hw : 2 * hw].astype(BF)
        dqb[:, 2 * hw : 3 * hw] = dv
        gbqkv[0:1, 2 * hw : 3 * hw] += col_sum(dv.astype(F32))

    def unproject(c):
        rows = pl.ds(c * CHUNK, CHUNK)
        red2.start(c, dot_nn(dqb[rows], wqkv[...]))

    def end(i, c):
        sl = pl.ds(c * piece, piece)
        e = red2.result(c)
        hat, inv = norm_stats(xinb[sl].astype(F32))
        add(0, col_sum(e * hat))
        add(1, col_sum(e))
        outb[sl] = (h1b[sl] + norm_back(e, hat, inv, vec[0:1, :])).astype(BF)

        @pl.when(stage == 1)
        def _():
            pipe_copy(i, c).start()

        @pl.when(stage == 0)
        def _():
            x_copy(i, c).start()

    def end_wait(i, c):
        @pl.when(stage == 1)
        def _():
            pipe_copy(i, c).wait_send()

        @pl.when(stage == 0)
        def _():
            x_copy(i, c).wait()

    @pl.when(stage == 1)
    def _():
        load.wait()

    def image(i, carry):
        ld = loads(i)
        for c in every:
            begin(i, c)
        for c in every:
            gatm.forward(c)
        for n in (5, 6):
            ld[n].wait()
        for c in every:
            feed(c)
            if c >= 1:
                red1.cross(c - 1)
        for n in (0, 1, 2, 3, 4, 7, 8):
            ld[n].wait()
        middle(i, 0)
        red1.cross(chunks - 1)
        for c in range(1, chunks - 1):
            middle(i, c)
        for c in every:
            gatm.drain(c)
        weights(g2, gb, dmb, HPAD)
        middle(i, chunks - 1)
        for c in every:
            gata.forward(c)
        weights(g1, slb, a2b, HPAD)
        for c in every:
            attend(c)
        close()
        for c in every:
            unproject(c)
            if c >= 1:
                red2.cross(c - 1)
        red2.cross(chunks - 1)
        for c in range(chunks - 1):
            end(i, c)
        weights(gout, ob, dab, HPAD)
        end(i, chunks - 1)
        weights(gqkv, dqb, a1b, HPAD)
        for c in every:
            gata.drain(c)
            red1.drain(c)
            red2.drain(c)
            end_wait(i, c)

        @pl.when(i + 1 < images)
        def _():
            for nx in loads(i + 1):
                nx.start()

        return carry

    lax.fori_loop(0, images, image, 0)


def vmem():
    return pl.BlockSpec(memory_space=pltpu.VMEM)


def anywhere():
    return pl.BlockSpec(memory_space=pl.ANY)


def comm_scratch(chunks, width, rows_mp):
    one = [
        pltpu.VMEM((chunks, CHUNK, width), BF),
        pltpu.VMEM((chunks, HALF, width), BF),
        pltpu.VMEM((chunks, rows_mp - 1, HALF // rows_mp, width), BF),
        pltpu.VMEM((chunks, rows_mp - 1, HALF // rows_mp, width), BF),
    ]
    return one + one


def sem_kinds(rows_mp):
    gather = 2 * rows_mp - 1
    return 0, gather, 2 * gather, 2 * gather + rows_mp


def sems(images, chunks, rows_mp):
    dma = pltpu.SemaphoreType.DMA
    kinds = 6 * rows_mp - 2
    return [dma((kinds, chunks)), dma((kinds, chunks)), dma((chunks,)), dma((images, chunks)), dma((10,))]


def on_device(
    section_in,
    ln1_gain,
    ln1_bias,
    qkv_weight,
    qv_bias,
    out_weight,
    out_bias,
    ln2_gain,
    ln2_bias,
    fc1_weight,
    fc1_bias,
    fc2_weight,
    fc2_bias,
):
    stage = lax.axis_index("pipe")
    me = lax.axis_index("mp")
    rows_in = section_in[0]
    images, length, width = rows_in.shape
    cols = out_weight.shape[1]
    heads = cols // HDIM
    hidden = fc1_weight.shape[2]
    hid = -(-hidden // HPAD) * HPAD
    chunks = -(-length // CHUNK)
    total = chunks * CHUNK
    hw = heads * HPAD
    scaling = HDIM ** (-0.5)
    rows_mp = lax.axis_size("mp") // 2
    piece = HALF // rows_mp
    pos = lax.rem(me, 2) * rows_mp + lax.div(me, 2)

    padded = jnp.pad(rows_in, ((0, 0), (0, total - length), (0, 0)))
    mine = lax.dynamic_index_in_dim(
        padded.reshape(images, chunks, 2 * rows_mp, piece, width), pos, 2, keepdims=False
    ).reshape(images, chunks * piece, width)

    def row_of(v):
        v = v.reshape(1, -1).astype(F32)
        return jnp.pad(v, ((0, 0), (0, width - v.shape[1])))

    vec = jnp.concatenate(
        [
            row_of(ln1_gain),
            row_of(ln1_bias),
            row_of(out_bias),
            row_of(ln2_gain),
            row_of(ln2_bias),
            row_of(fc1_bias),
            row_of(fc2_bias),
            jnp.zeros((1, width), F32),
        ]
    )
    lanes = ((0, 0), (0, 0), (0, 0), (0, HPAD - HDIM))
    tall = ((0, 0), (0, HPAD - HDIM), (0, 0))
    wqkv = jnp.transpose(qkv_weight[0], (1, 2, 0)).reshape(3 * heads, HDIM, width)
    wqkv = jnp.pad(wqkv, tall).reshape(3 * hw, width)
    bias_three = jnp.stack([qv_bias[0, 0], jnp.zeros_like(qv_bias[0, 0]), qv_bias[0, 1]])
    bqkv = jnp.pad(bias_three.reshape(1, 3, heads, HDIM), lanes).reshape(1, 3 * hw).astype(F32)
    wout = jnp.pad(out_weight[0].reshape(heads, HDIM, width), tall).reshape(hw, width)
    w1 = jnp.pad(fc1_weight[0].T, ((0, hid - hidden), (0, 0)))
    w2 = jnp.pad(fc2_weight[0], ((0, hid - hidden), (0, 0)))

    def arr(*shape, dtype=BF):
        return jax.ShapeDtypeStruct(shape, dtype)

    own = chunks * piece
    kept_shapes = [
        arr(images, own, width),
        arr(images, total, width),
        arr(images, total, 3 * hw),
        arr(images, total, hw),
        arr(images, total, HPAD, dtype=F32),
        arr(images, total, width),
        arr(images, total, hid),
        arr(images, total, hid),
        arr(images, own, width, dtype=F32),
    ]
    kept_vmem = [
        pltpu.VMEM((total, 3 * hw), BF),
        pltpu.VMEM((total, hw), BF),
        pltpu.VMEM((total, HPAD), F32),
        pltpu.VMEM((total, width), BF),
        pltpu.VMEM((total, hid), BF),
        pltpu.VMEM((total, hid), BF),
        pltpu.VMEM((own, width), F32),
    ]
    y_mine, *kept = pl.pallas_call(
        functools.partial(forward_kernel, images, chunks, heads, length, scaling, rows_mp),
        out_shape=[arr(images, own, width)] + kept_shapes,
        in_specs=[anywhere()] + [vmem()] * 6,
        out_specs=[anywhere()] * 10,
        scratch_shapes=[
            pltpu.VMEM((images, own, width), BF),
            pltpu.VMEM((2, total, width), BF),
            *kept_vmem,
            pltpu.VMEM((own, width), BF),
            *comm_scratch(chunks, width, rows_mp),
            *sems(images, chunks, rows_mp),
        ],
        compiler_params=pltpu.CompilerParams(
            collective_id=0, has_side_effects=True, vmem_limit_bytes=VMEM_LIMIT
        ),
        name="layer_forward",
    )(mine, vec, bqkv, wqkv, wout, w1, w2)

    dx_mine, gqkv, gout, g1, g2, small, gbqkv = pl.pallas_call(
        functools.partial(backward_kernel, images, chunks, heads, length, scaling, rows_mp),
        out_shape=[
            arr(images, own, width),
            arr(3 * hw, width, dtype=F32),
            arr(hw, width, dtype=F32),
            arr(hid, width, dtype=F32),
            arr(hid, width, dtype=F32),
            arr(8, width, dtype=F32),
            arr(1, 3 * hw, dtype=F32),
        ],
        in_specs=[anywhere()] + [vmem()] * 5 + [anywhere()] * 9,
        out_specs=[anywhere()] + [vmem()] * 6,
        scratch_shapes=[
            pltpu.VMEM((images, own, width), BF),
            pltpu.VMEM((own, width), BF),
            pltpu.VMEM((total, width), BF),
            *kept_vmem,
            pltpu.VMEM((total, width), BF),
            pltpu.VMEM((total, width), BF),
            pltpu.VMEM((total, 3 * hw), BF),
            pltpu.VMEM((total, 2 * hw), F32),
            pltpu.VMEM((CHUNK, hw), BF),
            pltpu.VMEM((own, width), BF),
            *comm_scratch(chunks, width, rows_mp),
            *sems(images, chunks, rows_mp),
        ],
        compiler_params=pltpu.CompilerParams(
            collective_id=1, has_side_effects=True, vmem_limit_bytes=VMEM_LIMIT
        ),
        name="layer_backward",
    )(mine, vec, wqkv, wout, w1, w2, *kept)

    out_mine = jnp.where(stage == 0, dx_mine, y_mine)
    whole = lax.all_gather(out_mine, "mp", axis=0)
    whole = whole.reshape(rows_mp, 2, images, chunks, piece, width)
    section_out = jnp.transpose(whole, (2, 3, 1, 0, 4, 5)).reshape(images, total, width)
    section_out = section_out[:, :length][None]

    gqkv = gqkv.reshape(3 * heads, HPAD, width)[:, :HDIM].reshape(3 * cols, width)
    gout = gout.reshape(heads, HPAD, width)[:, :HDIM].reshape(cols, width)
    stack = jnp.concatenate([g.astype(BF) for g in (gqkv, gout, g1[:hidden], g2[:hidden])])
    part = lax.psum_scatter(stack, "dp", scatter_dimension=1, tiled=True)
    stack = lax.all_gather(part, "dp", axis=1, tiled=True).astype(F32)
    gqkv, gout = stack[: 3 * cols], stack[3 * cols : 4 * cols]
    g1, g2 = stack[4 * cols : 4 * cols + hidden].T, stack[4 * cols + hidden :]
    gqkv = jnp.transpose(gqkv.reshape(3, cols, width), (2, 0, 1))
    gb = gbqkv.reshape(3, heads, HPAD)[:, :, :HDIM].reshape(3, cols)
    local = lax.psum((gb, small[5, :hidden]), "dp")
    wide = lax.psum(small, ("dp", "mp"))
    return (
        section_out,
        wide[0][None],
        wide[1][None],
        gqkv[None],
        jnp.stack([local[0][0], local[0][2]])[None],
        gout[None],
        wide[2][None],
        wide[3][None],
        wide[4][None],
        g1[None],
        local[1][None],
        g2[None],
        wide[6][None],
    )


def solution(mesh):
    vector, matrix = P("pipe", None), P("pipe", "mp", None)
    acts = P("pipe", "dp", None, None)
    heads = P("pipe", None, None, "mp")
    pair = P("pipe", None, "mp")
    params = (vector, vector, heads, pair, matrix, vector, vector, vector, pair, P("pipe", "mp"), matrix, vector)
    return jax.shard_map(
        on_device,
        mesh=mesh,
        in_specs=(acts, *params),
        out_specs=(acts, *params),
        check_vma=False,
    )
```

time: 1640 us -> 976 us (0.60)
  waiting for transfers between devices: 980 us -> 173 us
  Pallas kernels: 0 us -> 537 us
  matrix products: 304 us -> 0 us
  other arithmetic: 195 us -> 11.8 us
  local copies, waits for them, and re-layouts: 72 us -> 144 us
  blocking collectives: 41.1 us -> 89.2 us
  starting transfers between devices: 19.7 us -> 0.13 us
    psum x11 -> x0, waiting for transfers between devices: 581 us -> none  [the longest x4 229 us: layer_backward(): lax.psum(jnp.einsum('sc,dc->sd', d_packed, w_qkv, preferred_element_type=...]
    pallas_call x0 -> x2, Pallas kernels: none -> 537 us  [the longest x1 355 us: on_device(): pl.pallas_call(functools.partial(backward_kernel, images, chunks, heads,...]
    dot_general x76 -> x0, matrix products: 304 us -> none  [the longest x4 55.3 us: layer_forward(): jnp.dot(act_out.astype(jnp.bfloat16), w_fc2, preferred_element_type=jnp.f...]
    ppermute x6 -> x0, waiting for transfers between devices: 199 us -> none  [shifted(): return lax.ppermute(value, axis, pairs)]
    reduce_sum x44 -> x0, other arithmetic: 104 us -> none  [the longest x14 38.2 us: norm_rows(): center = values - jnp.mean(values, axis=-1, keepdims=True)]
    unnamed x19 -> x4, waiting for transfers between devices: 26.4 us -> 130 us
    all_gather x3 -> x2, waiting for transfers between devices: 124 us -> 42.7 us  [the longest x1 42.7 us: on_device(): stack = lax.all_gather(part, 'dp', axis=1, tiled=True).astype(F32)]
    psum x1 -> x2, blocking collectives: 22.3 us -> 89.2 us  [the longest x1 70.1 us: on_device(): wide = lax.psum(small, ('dp', 'mp'))]
  transfers between devices with their start and end apart: 24 -> 3, of which waited for: 23 -> 2; matrix products, arithmetic and copies ran while one was open for 10% -> 1% of each run, Pallas kernels for 0% -> 0%
where the time goes in v1:
time: 976 us; the launch traced here: 971 us
  Pallas kernels  537 us (55%)
  waiting for transfers between devices  173 us (18%)
  local copies, waits for them, and re-layouts  144 us (15%)
  blocking collectives  89.2 us (9%)
  between operations  16.1 us (2%)
  other arithmetic  11.8 us (1%)
    pallas_call x1, Pallas kernels, on_device(): pl.pallas_call(functools.partial(backward_kernel, images, chunks, heads,...  355 us
    pallas_call x1, Pallas kernels, on_device(): pl.pallas_call(functools.partial(forward_kernel, images, chunks, heads, l...  182 us
    unnamed x4, waiting for transfers between devices  130 us
    psum x1, blocking collectives, on_device(): wide = lax.psum(small, ('dp', 'mp'))  70.1 us
    unnamed x37, local copies, waits for them, and re-layouts  58.8 us
    all_gather x1, waiting for transfers between devices, on_device(): stack = lax.all_gather(part, 'dp', axis=1, tiled=True).astype(F32)  42.7 us
    concatenate x1, local copies, waits for them, and re-layouts, on_device(): jnp.concatenate([g.astype(BF) for g in (gqkv, gout, g1[:hidden], g2[:hidd...  30.9 us
  transfers between devices with their start and end apart: 3, of which 2 were waited for; matrix products, arithmetic and copies ran while one was open for 1% of the time, Pallas kernels for 0%

profile of v1, /device:TPU:0, one launch (start us, length us, event | category | flops | bytes accessed | tf_op | source)
XLA Modules:
  0.0 970.9 jit_solution(7005433252438752255)
XLA Ops:
  8.0 0.0 reduce-scatter.4.cloned.1.call-start
  8.1 0.9 slice_reduce_fusion.1
  8.9 0.1 stack.10
  9.0 0.1 stack.11
  9.1 0.1 pad.41.clone
  9.2 0.1 pad_maximum_fusion
  9.3 0.6 pad_convert_fusion.1
  9.9 0.7 pad_convert_fusion
  10.6 2.2 pad.34
  12.8 3.6 pad.35.w1
  16.3 1.7 pad.36.w2
  18.0 2.3 pad.33
  20.4 2.8 pad.30
  23.1 2.5 constant_dynamic-slice_fusion
  25.7 0.7 concatenate.7.vec
  26.3 182.4 %layer_forward.1 = (bf16[3,192,1152]{2,1,0:T(8,128)(2,1)}, bf16[3,192,1152]{2,1,0:T(8,128)(2,1)}, bf16[3,768,1152]{2,1,0:T(8,128)(2,1)}, bf16[3,768,1536]{2,1,0:...) custom-call(bf16[3,192,1152]{2,1,0:T(8,128)(2,1)} %bitcast.52, ...), custom_call_target="tpu_custom_call" | custom-call | tf_op jit(solution)/shard_map/layer_forward/pallas_call | solution.py:742
  208.7 355.1 %layer_backward.1 = (bf16[3,192,1152]{2,1,0:T(8,128)(2,1)}, f32[1536,1152]{1,0:T(8,128)}, f32[512,1152]{1,0:T(8,128)}, f32[1152,1152]{1,0:T(8,128)}, f32[1152,11...) custom-call(bf16[3,192,1152]{2,1,0:T(8,128)(2,1)} %bitcast.53, f32[8,1152]{1,0:T(8,128)} %concatenate.7.vec, ...), custom_call_target="tpu_custom_call" | custom-call | tf_op jit(solution)/shard_map/layer_backward/pallas_call | solution.py:761
  563.9 1.9 convert.18
  565.8 0.1 slice.92
  565.9 2.8 slice.115
  568.7 4.1 slice.114
  572.8 0.4 convert.17
  573.2 1.5 slice.91
  574.6 30.9 %concatenate.8 = bf16[3304,1152]{1,0:T(8,128)(2,1)} concatenate(bf16[864,1152]{1,0:T(8,128)(2,1)} %bitcast.58, bf16[288,1152]{1,0:T(8,128)(2,1)S(1)} %bitcast.67, bf16[1076,1152]{1,0:T(8,128)(2,1)S(1)} %slice.115, bf16[1076,1152]{1,0:T(8,128)(2,1)} %slice.114), dimensions={0} | concatenate | bytes 15224832 | tf_op jit(solution)/shard_map/concatenate | solution.py:802
  605.6 11.5 %copy.43 = bf16[3304,1152]{0,1:T(8,128)(2,1)} copy(bf16[3304,1152]{1,0:T(8,128)(2,1)} %concatenate.8) | data formatting | bytes 15224832
  617.1 0.0 all-gather.6.cloned.1.call-start
  617.2 1.2 copy-done.3
  618.4 0.4 copy-done.4
  618.8 1.2 broadcast_select_fusion
  620.0 0.0 all-gather.6.cloned.1.call-update
  620.0 0.0 all-gather.4.cloned.1.call-start
  620.1 129.7 %reduce-scatter.4.cloned.1.call-done = bf16[288,3304]{1,0:T(8,128)(2,1)} async-done(((bf16[1152,3304]{1,0:T(8,128)(2,1)}), bf16[288,3304]{1,0:T(8,128)(2,1)}) %reduce-scatter.4.cloned.1.call-update) | async-done | bytes 1903120
  749.9 0.1 reshape.101
  750.0 19.1 %all-reduce.7 = (f32[3,288]{1,0:T(4,128)S(1)}, f32[1,1076]{1,0:T(1,128)}) all-reduce(f32[3,288]{1,0:T(4,128)S(1)} %reshape.101, f32[1,1076]{1,0:T(1,128)S(1)} %slice.85), channel_id=1, replica_groups=mesh['pipe'=2,'dp'=4,'mp'=4] {'dp'}, use_global_device_ids=true, to_apply=%region_2.3 | all-reduce | flops 1940 | bytes 15520 | tf_op jit(solution)/shard_map/psum | solution.py:809
  769.0 70.1 %psum.21 = f32[8,1152]{1,0:T(8,128)S(1)} all-reduce(f32[8,1152]{1,0:T(8,128)S(1)} %copy-done.5), channel_id=1, replica_groups=mesh['pipe'=2,'dp'=4,'mp'=4] {'dp','mp'}, use_global_device_ids=true, to_apply=%region_0.1 | all-reduce | flops 9216 | bytes 73728 | tf_op jit(solution)/shard_map/psum | solution.py:810
  839.1 0.6 maximum_bitcast_fusion
  839.7 0.6 fusion
  840.3 3.0 copy.38
  843.4 2.7 slice_bitcast_fusion
  846.1 42.7 %all-gather.4.cloned.1.call-done = bf16[3304,1152]{0,1:T(8,128)(2,1)} async-done(((bf16[3304,288]{0,1:T(8,128)(2,1)}), bf16[3304,1152]{0,1:T(8,128)(2,1)}) %all-gather.4.cloned.1.call-update) | async-done | bytes 7612432 | tf_op jit(solution)/shard_map/all_gather | solution.py:804
  888.8 11.4 %copy.40 = bf16[3304,1152]{1,0:T(8,128)(2,1)} copy(bf16[3304,1152]{0,1:T(8,128)(2,1)} %all-gather.4.cloned.1.call-done) | data formatting | bytes 15224832 | tf_op jit(solution)/shard_map/all_gather | solution.py:804
  900.2 4.0 slice.95
  904.2 1.2 copy-done
  905.4 6.3 convert_element_type.60
  911.7 2.5 slice_bitcast_fusion.3
  914.2 4.6 slice_bitcast_fusion.1
  918.7 22.2 %copy.42 = f32[1,1076,1152]{2,0,1:T(1,128)} copy(f32[1,1076,1152]{2,1,0:T(8,128)S(1)} %get-tuple-element.90) | data formatting | bytes 9916416
  941.0 22.2 %copy.41 = f32[1,1152,1076]{1,0,2:T(1,128)} copy(f32[1,1152,1076]{1,2,0:T(8,128)S(1)} %get-tuple-element.91) | data formatting | bytes 9916416
  (39 shorter events, 0.1 us)
Async XLA Ops:
  8.0 8.3 copy-start.1
  8.0 741.8 %reduce-scatter.4.cloned.1.call-start = ((), (), s32[]{:S(2)}) async-start(), calls=%async_computation.3 | async-start | bytes 9584640
  12.8 5.3 copy-start.2
  12.8 7.5 slice-start.2
  16.3 4.0 slice-start.3
  20.3 5.3 copy-start.7
  20.3 5.3 copy-start.8
  20.3 5.3 copy-start.9
  20.3 5.3 copy-start.10
  20.3 5.3 copy-start.11
  20.3 5.3 copy-start.12
  563.9 9.0 slice-start
  565.9 6.9 slice-start.1
  617.1 1.3 copy-start.3
  617.1 1.7 copy-start.4
  617.1 132.8 %copy-start.5 = (f32[8,1152]{1,0:T(8,128)S(1)}, f32[8,1152]{1,0:T(8,128)}, u32[]{:S(2)}) copy-start(f32[8,1152]{1,0:T(8,128)} %get-tuple-element.41) | copy-start | bytes 110596
  617.1 132.8 %copy-start.6 = (f32[1,1536]{1,0:T(1,128)S(1)}, f32[1,1536]{1,0:T(1,128)}, u32[]{:S(2)}) copy-start(f32[1,1536]{1,0:T(1,128)} %get-tuple-element.46) | copy-start | bytes 18436
  617.1 223.2 %all-gather.6.cloned.1.call-start = ((), (), s32[]{:S(2)}) async-start(), calls=%async_computation.2 | async-start | bytes 6635520 | tf_op jit(solution)/shard_map/all_gather | solution.py:795
  620.0 268.8 %all-gather.4.cloned.1.call-start = ((), (), s32[]{:S(2)}) async-start(), calls=%async_computation.1 | async-start | bytes 9584640 | tf_op jit(solution)/shard_map/all_gather | solution.py:804
  900.2 5.2 copy-start
Sparse Core Ops, SparseCore 0:
  617.2 132.5 reduce-scatter.3
Sparse Core Ops, SparseCore 1:
  620.1 40.1 all-gather.5
  749.9 138.8 all-gather.3

commit v2 on v1

--- a/solution.py
+++ b/solution.py
@@ -18,6 +18,10 @@
 CHUNK = 256
 HALF = CHUNK // 2
 VMEM_LIMIT = 67043328
+SKEW = 2
+SLOTS = 4
+PART_SLOTS = 8
+SUM_SLOTS = 8
 
 
 def dot_nn(a, b):
@@ -69,10 +73,16 @@
         return {"mp": row * 2 + self.core}
 
 
-def enter(spot):
+def others(axis, count):
+    me = lax.axis_index(axis)
+    return [lax.rem(me + j, count) for j in range(1, count)]
+
+
+def enter(spot, dp_n=1):
     barrier = pltpu.get_barrier_semaphore()
-    targets = [{"mp": spot.sib}, {"pipe": 1 - spot.stage}]
-    targets += [spot.peer(spot.ahead(j)) for j in range(1, spot.rows)]
+    targets = [{"pipe": 1 - spot.stage}]
+    targets += [{"mp": t} for t in others("mp", 2 * spot.rows)]
+    targets += [{"dp": t} for t in others("dp", dp_n)]
     for target in targets:
         pl.semaphore_signal(barrier, inc=1, device_id=target, device_id_type=MESH)
     pl.semaphore_wait(barrier, len(targets))
@@ -394,22 +404,27 @@
 
 
 def backward_kernel(
-    images, chunks, heads, length, scaling, rows_mp,
-    d_hbm, vec, wqkv, wout, w1, w2,
+    images, chunks, heads, length, scaling, rows_mp, dp_n, pairs,
+    d_hbm, y_in, vec, wqkv, wout, w1, w2,
     xin_i, a1_i, qkv_i, o_i, lse_i, a2_i, g_i, sl_i, h1_i,
-    dx_o, gqkv, gout, g1, g2, small, gbqkv,
-    dbuf, xinb, a1b, qkvb, ob, lseb, a2b, gb, slb, h1b, dmb, dab, dqb, dkv, dob, outb,
-    part1, near1, out1, far1, part2, near2, out2, far2,
-    ssem, rsem, psend, precv, lsem,
+    full_o, fin, sums_o,
+    acc, small, gbqkv, obuf, fbuf, stage_buf, land_buf, sum_buf, mslot, dslot, sbuf, dbuf, xinb, a1b, qkvb, ob, lseb, a2b, gb, slb, h1b, dmb, dab, dqb, dkv, dob, outb,
+    part1, near1, out1, far1,
+    ssem, rsem, psend, precv, lsem, agsend, agrecv, msem, mrecv, dsem, drecv, zsend, zpart, zfinal, zpass, zkeep, pcredit, fcredit,
 ):
     spot = Spot(rows_mp)
     stage, piece = spot.stage, spot.piece
     hw = heads * HPAD
+    hid = w1.shape[0]
+    z = lax.axis_index("dp")
+    me = lax.axis_index("mp")
     load = pltpu.make_async_copy(d_hbm, dbuf, lsem.at[0])
+    load_y = pltpu.make_async_copy(y_in, obuf, lsem.at[10])
 
     @pl.when(stage == 1)
     def _():
         load.start()
+        load_y.start()
 
     def loads(i):
         return [
@@ -431,18 +446,15 @@
 
     for ld in loads(0):
         ld.start()
-    enter(spot)
+    enter(spot, dp_n)
     kinds = sem_kinds(rows_mp)
     gatm = Gather(dmb, ssem, rsem, kinds[0], spot)
     gata = Gather(dab, ssem, rsem, kinds[1], spot)
     red1 = Reduce(part1, near1, out1, far1, ssem, rsem, kinds[2], spot)
-    red2 = Reduce(part2, near2, out2, far2, ssem, rsem, kinds[3], spot)
+    red2 = Reduce(part1, near1, out1, far1, ssem, rsem, kinds[3], spot)
     every = range(chunks)
 
-    gqkv[...] = jnp.zeros_like(gqkv)
-    gout[...] = jnp.zeros_like(gout)
-    g1[...] = jnp.zeros_like(g1)
-    g2[...] = jnp.zeros_like(g2)
+    acc[...] = jnp.zeros_like(acc)
     small[...] = jnp.zeros_like(small)
     gbqkv[...] = jnp.zeros_like(gbqkv)
 
@@ -456,11 +468,6 @@
             psend.at[c],
             precv.at[i, c],
             {"pipe": 0},
-        )
-
-    def x_copy(i, c):
-        return pltpu.make_async_copy(
-            outb.at[pl.ds(c * piece, piece)], dx_o.at[i, pl.ds(c * piece, piece)], psend.at[c]
         )
 
     def begin(i, c):
@@ -493,13 +500,13 @@
         gata.mine(c)[...] = dh.astype(BF)
         gata.start(c)
 
-    def weights(acc, a, b, step):
+    def weights(base, a, b, step):
         def tile(n, carry):
             cols = pl.ds(pl.multiple_of(n * step, step), step)
-            acc[cols] += dot_tn(a[:, cols], b[...])
+            acc[pl.ds(pl.multiple_of(base + n * step, step), step)] += dot_tn(a[:, cols], b[...])
             return carry
 
-        lax.fori_loop(0, acc.shape[0] // step, tile, 0)
+        lax.fori_loop(0, a.shape[1] // step, tile, 0)
 
     def attend(c):
         rows = pl.ds(c * CHUNK, CHUNK)
@@ -547,28 +554,26 @@
         hat, inv = norm_stats(xinb[sl].astype(F32))
         add(0, col_sum(e * hat))
         add(1, col_sum(e))
-        outb[sl] = (h1b[sl] + norm_back(e, hat, inv, vec[0:1, :])).astype(BF)
+        dx = (h1b[sl] + norm_back(e, hat, inv, vec[0:1, :])).astype(BF)
 
         @pl.when(stage == 1)
         def _():
+            outb[sl] = dx
             pipe_copy(i, c).start()
 
         @pl.when(stage == 0)
         def _():
-            x_copy(i, c).start()
+            obuf[i, c] = dx
 
     def end_wait(i, c):
         @pl.when(stage == 1)
         def _():
             pipe_copy(i, c).wait_send()
-
-        @pl.when(stage == 0)
-        def _():
-            x_copy(i, c).wait()
 
     @pl.when(stage == 1)
     def _():
         load.wait()
+        load_y.wait()
 
     def image(i, carry):
         ld = loads(i)
@@ -590,14 +595,16 @@
             middle(i, c)
         for c in every:
             gatm.drain(c)
-        weights(g2, gb, dmb, HPAD)
+        weights(0, gb, dmb, HPAD)
         middle(i, chunks - 1)
         for c in every:
             gata.forward(c)
-        weights(g1, slb, a2b, HPAD)
+        weights(hid, slb, a2b, HPAD)
         for c in every:
             attend(c)
         close()
+        for c in every:
+            red1.drain(c)
         for c in every:
             unproject(c)
             if c >= 1:
@@ -605,12 +612,11 @@
         red2.cross(chunks - 1)
         for c in range(chunks - 1):
             end(i, c)
-        weights(gout, ob, dab, HPAD)
+        weights(2 * hid, ob, dab, HPAD)
         end(i, chunks - 1)
-        weights(gqkv, dqb, a1b, HPAD)
+        weights(2 * hid + hw, dqb, a1b, HPAD)
         for c in every:
             gata.drain(c)
-            red1.drain(c)
             red2.drain(c)
             end_wait(i, c)
 
@@ -622,6 +628,255 @@
         return carry
 
     lax.fori_loop(0, images, image, 0)
+
+    def block(core, row):
+        return full_o.at[:, :, core * rows_mp + row]
+
+    ag_own = pltpu.make_async_copy(obuf, block(spot.core, spot.row), lsem.at[0])
+
+    def ag_near():
+        return remote(obuf, block(spot.core, spot.row), agsend.at[0], agrecv.at[0], {"mp": spot.sib})
+
+    def ag_far(j):
+        k = 2 * j - 1
+        return remote(obuf, fbuf.at[j - 1], agsend.at[k], agrecv.at[k], spot.peer(spot.ahead(j)))
+
+    def ag_pass(j):
+        view = block(spot.core, spot.behind(j))
+        return remote(fbuf.at[j - 1], view, agsend.at[2 * j], agrecv.at[2 * j], {"mp": spot.sib})
+
+    def ag_keep(j):
+        return pltpu.make_async_copy(fbuf.at[j - 1], block(spot.core, spot.behind(j)), lsem.at[3 + j])
+
+    ag_own.start()
+    for j in range(1, rows_mp):
+        ag_far(j).start()
+    ag_near().start()
+
+    mp_n = 2 * rows_mp
+
+    def mp_copy(j):
+        return remote(small, mslot.at[me], msem.at[j - 1], mrecv.at[j - 1], {"mp": lax.rem(me + j, mp_n)})
+
+    def dp_copy(j):
+        return remote(sbuf, dslot.at[z], dsem.at[j - 1], drecv.at[j - 1], {"dp": lax.rem(z + j, dp_n)})
+
+    for j in range(1, mp_n):
+        mp_copy(j).start()
+    mslot[me] = small[...]
+    for j in range(1, mp_n):
+        mp_copy(j).wait_recv()
+    total = mslot[0]
+    for j in range(1, mp_n):
+        total = total + mslot[j]
+    own_row = lax.broadcasted_iota(jnp.int32, total.shape, 0) == 5
+    sbuf[0:8] = jnp.where(own_row, small[...], total)
+    sbuf[8:16] = jnp.zeros_like(total)
+    sbuf[8:9, 0:hw] = gbqkv[0:1, 0:hw]
+    sbuf[9:10, 0:hw] = gbqkv[0:1, 2 * hw : 3 * hw]
+    for j in range(1, dp_n):
+        dp_copy(j).start()
+    dslot[z] = sbuf[...]
+
+    tall = stage_buf.shape[1]
+    units = fin.shape[0]
+    wide_units = 2 * pairs
+    right, left = lax.rem(z + 1, dp_n), lax.rem(z + dp_n - 1, dp_n)
+
+    def owner(u):
+        return dp_n // 2 - 1 + lax.rem(u, 2)
+
+    def send_copy(dst, u, side, recv):
+        slot = lax.rem(u, SLOTS)
+        return remote(stage_buf.at[slot], dst, zsend.at[slot, side], recv, {"dp": left if side else right})
+
+    def part_copy(u, side):
+        slot = lax.rem(u, PART_SLOTS)
+        return send_copy(land_buf.at[side, slot], u, side, zpart.at[side, slot])
+
+    def sum_copy(u, side):
+        slot = lax.rem(u, SUM_SLOTS)
+        return send_copy(sum_buf.at[slot], u, side, zfinal.at[slot])
+
+    def keep_copy(u):
+        slot = lax.rem(u, SLOTS)
+        return pltpu.make_async_copy(stage_buf.at[slot], fin.at[u], zsend.at[slot, 2])
+
+    def pass_copy(u, side):
+        slot = lax.rem(u, SUM_SLOTS)
+        view = sum_buf.at[slot]
+        return remote(view, view, zpass.at[slot], zfinal.at[slot], {"dp": left if side else right})
+
+    def write_copy(u):
+        slot = lax.rem(u, SUM_SLOTS)
+        return pltpu.make_async_copy(sum_buf.at[slot], fin.at[u], zkeep.at[slot])
+
+    def grant(sem, target):
+        pl.semaphore_signal(sem, inc=1, device_id={"dp": target}, device_id_type=MESH)
+
+    def sends(u, act):
+        mid = owner(u)
+
+        @pl.when((z <= mid) & (z < dp_n - 1))
+        def _():
+            act(0)
+
+        @pl.when((z >= mid) & (z > 0))
+        def _():
+            act(1)
+
+    def settle(u):
+        sends(u, lambda side: part_copy(u, side).wait_send())
+
+        @pl.when(z == owner(u))
+        def _():
+            keep_copy(u).wait()
+
+    def start_sum(copy, u, side):
+        @pl.when(u >= SUM_SLOTS)
+        def _():
+            pl.semaphore_wait(fcredit.at[side, lax.rem(u, 2)], 1)
+
+        copy.start()
+
+    def start_part(u, side):
+        @pl.when(u >= PART_SLOTS)
+        def _():
+            pl.semaphore_wait(pcredit.at[side, lax.rem(u, 2)], 1)
+
+        part_copy(u, side).start()
+
+    def reduce_unit(u, value):
+        mid = owner(u)
+        from_left = (z > 0) & (z <= mid)
+        from_right = (z < dp_n - 1) & (z >= mid)
+        for side, cond in ((0, from_left), (1, from_right)):
+
+            @pl.when(cond)
+            def _(side=side):
+                part_copy(u, side).wait_recv()
+
+            value = value + jnp.where(cond, land_buf[side, lax.rem(u, PART_SLOTS)].astype(F32), 0.0)
+
+        @pl.when(u >= SLOTS)
+        def _():
+            settle(u - SLOTS)
+
+        stage_buf[lax.rem(u, SLOTS)] = value.astype(BF)
+        for side, cond in ((0, from_left), (1, from_right)):
+
+            @pl.when(cond & (u + PART_SLOTS < units))
+            def _(side=side):
+                grant(pcredit.at[side, lax.rem(u, 2)], right if side else left)
+
+        @pl.when(z == mid)
+        def _():
+            keep_copy(u).start()
+            sends(u, lambda side: start_sum(sum_copy(u, side), u, side))
+
+        @pl.when(z != mid)
+        def _():
+            sends(u, lambda side: start_part(u, side))
+
+    def release(u):
+        mid = owner(u)
+        write_copy(u).wait()
+
+        @pl.when(((z < mid) & (z > 0)) | ((z > mid) & (z < dp_n - 1)))
+        def _():
+            pass_copy(u, 0).wait_send()
+
+        @pl.when((z < mid) & (u + SUM_SLOTS < units))
+        def _():
+            grant(fcredit.at[1, lax.rem(u, 2)], right)
+
+        @pl.when((z > mid) & (u + SUM_SLOTS < units))
+        def _():
+            grant(fcredit.at[0, lax.rem(u, 2)], left)
+
+    def spread_unit(u):
+        mid = owner(u)
+
+        @pl.when(z != mid)
+        def _():
+            sum_copy(u, 0).wait_recv()
+            write_copy(u).start()
+
+            @pl.when((z < mid) & (z > 0))
+            def _():
+                start_sum(pass_copy(u, 1), u, 1)
+
+            @pl.when((z > mid) & (z < dp_n - 1))
+            def _():
+                start_sum(pass_copy(u, 0), u, 0)
+
+            @pl.when(u >= 2)
+            def _():
+                release(u - 2)
+
+    half = dp_n // 2
+
+    def unit(t, carry):
+        mid = owner(t)
+        late = t - SKEW * (half + jnp.abs(z - mid))
+        now = t - SKEW * jnp.where(z < mid, z, jnp.where(z > mid, dp_n - 1 - z, half))
+
+        @pl.when((z != mid) & (late >= 0) & (late < units))
+        def _():
+            spread_unit(late)
+
+        @pl.when((now >= 0) & (now < wide_units))
+        def _():
+            start = now * tall + lax.div(now, pairs) * (hid - pairs * tall)
+            reduce_unit(now, acc[pl.ds(pl.multiple_of(start, 8), tall)])
+
+        @pl.when((now >= wide_units) & (now < units))
+        def _():
+            start = 2 * hid + (now - wide_units) * HPAD
+            reduce_unit(now, acc[pl.ds(pl.multiple_of(start, HPAD), tall)])
+
+        return carry
+
+    lax.fori_loop(0, 8, unit, 0)
+    for j in range(1, dp_n):
+        dp_copy(j).wait_recv()
+    total = dslot[0]
+    for j in range(1, dp_n):
+        total = total + dslot[j]
+    sums_o[...] = total
+    lax.fori_loop(8, 16, unit, 0)
+    for j in range(1, rows_mp):
+        ag_far(j).wait_recv()
+        ag_pass(j).start()
+        ag_keep(j).start()
+    lax.fori_loop(16, units + SKEW * dp_n, unit, 0)
+
+    def last(t, carry):
+        settle(t)
+        return carry
+
+    lax.fori_loop(units - SLOTS, units, last, 0)
+
+    def freed(u, carry):
+        @pl.when(z != owner(u))
+        def _():
+            release(u)
+
+        return carry
+
+    lax.fori_loop(units - 2, units, freed, 0)
+    ag_own.wait()
+    ag_near().wait_send()
+    ag_near().wait_recv()
+    for j in range(1, rows_mp):
+        ag_far(j).wait_send()
+        ag_pass(j).wait_send()
+        ag_pass(j).wait_recv()
+        ag_keep(j).wait()
+    for j in range(1, mp_n):
+        mp_copy(j).wait_send()
+    for j in range(1, dp_n):
+        dp_copy(j).wait_send()
 
 
 def vmem():
@@ -650,7 +905,7 @@
 def sems(images, chunks, rows_mp):
     dma = pltpu.SemaphoreType.DMA
     kinds = 6 * rows_mp - 2
-    return [dma((kinds, chunks)), dma((kinds, chunks)), dma((chunks,)), dma((images, chunks)), dma((10,))]
+    return [dma((kinds, chunks)), dma((kinds, chunks)), dma((chunks,)), dma((images, chunks)), dma((11,))]
 
 
 def on_device(
@@ -758,20 +1013,32 @@
         name="layer_forward",
     )(mine, vec, bqkv, wqkv, wout, w1, w2)
 
-    dx_mine, gqkv, gout, g1, g2, small, gbqkv = pl.pallas_call(
-        functools.partial(backward_kernel, images, chunks, heads, length, scaling, rows_mp),
+    dp_n = lax.axis_size("dp")
+    tall_unit = HDIM
+    pairs = -(-hidden // tall_unit)
+    units = 2 * pairs + 4 * heads
+    dma = pltpu.SemaphoreType.DMA
+    full, fin, sums = pl.pallas_call(
+        functools.partial(backward_kernel, images, chunks, heads, length, scaling, rows_mp, dp_n, pairs),
         out_shape=[
-            arr(images, own, width),
-            arr(3 * hw, width, dtype=F32),
-            arr(hw, width, dtype=F32),
-            arr(hid, width, dtype=F32),
-            arr(hid, width, dtype=F32),
-            arr(8, width, dtype=F32),
-            arr(1, 3 * hw, dtype=F32),
+            arr(images, chunks, 2 * rows_mp, piece, width),
+            arr(units, tall_unit, width),
+            arr(16, width, dtype=F32),
         ],
-        in_specs=[anywhere()] + [vmem()] * 5 + [anywhere()] * 9,
-        out_specs=[anywhere()] + [vmem()] * 6,
+        in_specs=[anywhere()] * 2 + [vmem()] * 5 + [anywhere()] * 9,
+        out_specs=[anywhere()] * 2 + [vmem()],
         scratch_shapes=[
+            pltpu.VMEM((2 * hid + 4 * hw, width), F32),
+            pltpu.VMEM((8, width), F32),
+            pltpu.VMEM((1, 3 * hw), F32),
+            pltpu.VMEM((images, chunks, piece, width), BF),
+            pltpu.VMEM((rows_mp - 1, images, chunks, piece, width), BF),
+            pltpu.VMEM((SLOTS, tall_unit, width), BF),
+            pltpu.VMEM((2, PART_SLOTS, tall_unit, width), BF),
+            pltpu.VMEM((SUM_SLOTS, tall_unit, width), BF),
+            pltpu.VMEM((2 * rows_mp, 8, width), F32),
+            pltpu.VMEM((dp_n, 16, width), F32),
+            pltpu.VMEM((16, width), F32),
             pltpu.VMEM((images, own, width), BF),
             pltpu.VMEM((own, width), BF),
             pltpu.VMEM((total, width), BF),
@@ -782,46 +1049,53 @@
             pltpu.VMEM((total, 2 * hw), F32),
             pltpu.VMEM((CHUNK, hw), BF),
             pltpu.VMEM((own, width), BF),
-            *comm_scratch(chunks, width, rows_mp),
+            *comm_scratch(chunks, width, rows_mp)[:4],
             *sems(images, chunks, rows_mp),
+            dma((2 * rows_mp - 1,)),
+            dma((2 * rows_mp - 1,)),
+            dma((2 * rows_mp - 1,)),
+            dma((2 * rows_mp - 1,)),
+            dma((dp_n - 1,)),
+            dma((dp_n - 1,)),
+            dma((SLOTS, 3)),
+            dma((2, PART_SLOTS)),
+            dma((SUM_SLOTS,)),
+            dma((SUM_SLOTS,)),
+            dma((SUM_SLOTS,)),
+            pltpu.SemaphoreType.REGULAR((2, 2)),
+            pltpu.SemaphoreType.REGULAR((2, 2)),
         ],
         compiler_params=pltpu.CompilerParams(
             collective_id=1, has_side_effects=True, vmem_limit_bytes=VMEM_LIMIT
         ),
         name="layer_backward",
-    )(mine, vec, wqkv, wout, w1, w2, *kept)
-
-    out_mine = jnp.where(stage == 0, dx_mine, y_mine)
-    whole = lax.all_gather(out_mine, "mp", axis=0)
-    whole = whole.reshape(rows_mp, 2, images, chunks, piece, width)
-    section_out = jnp.transpose(whole, (2, 3, 1, 0, 4, 5)).reshape(images, total, width)
-    section_out = section_out[:, :length][None]
-
-    gqkv = gqkv.reshape(3 * heads, HPAD, width)[:, :HDIM].reshape(3 * cols, width)
-    gout = gout.reshape(heads, HPAD, width)[:, :HDIM].reshape(cols, width)
-    stack = jnp.concatenate([g.astype(BF) for g in (gqkv, gout, g1[:hidden], g2[:hidden])])
-    part = lax.psum_scatter(stack, "dp", scatter_dimension=1, tiled=True)
-    stack = lax.all_gather(part, "dp", axis=1, tiled=True).astype(F32)
-    gqkv, gout = stack[: 3 * cols], stack[3 * cols : 4 * cols]
-    g1, g2 = stack[4 * cols : 4 * cols + hidden].T, stack[4 * cols + hidden :]
+    )(mine, y_mine.reshape(images, chunks, piece, width), vec, wqkv, wout, w1, w2, *kept)
+
+    section_out = full.reshape(images, total, width)[:, :length][None]
+    rows = fin.reshape(units * tall_unit, width)
+
+    def take(start, count):
+        return rows[start : start + count].astype(F32)
+
+    base = 2 * pairs * tall_unit
+    g2, g1 = take(0, hidden), take(pairs * tall_unit, hidden).T
+    gout, gqkv = take(base, cols), take(base + cols, 3 * cols)
     gqkv = jnp.transpose(gqkv.reshape(3, cols, width), (2, 0, 1))
-    gb = gbqkv.reshape(3, heads, HPAD)[:, :, :HDIM].reshape(3, cols)
-    local = lax.psum((gb, small[5, :hidden]), "dp")
-    wide = lax.psum(small, ("dp", "mp"))
+    gb = sums[8:10, :hw].reshape(2, heads, HPAD)[:, :, :HDIM].reshape(1, 2, cols)
     return (
         section_out,
-        wide[0][None],
-        wide[1][None],
+        sums[0:1],
+        sums[1:2],
         gqkv[None],
-        jnp.stack([local[0][0], local[0][2]])[None],
+        gb,
         gout[None],
-        wide[2][None],
-        wide[3][None],
-        wide[4][None],
+        sums[2:3],
+        sums[3:4],
+        sums[4:5],
         g1[None],
-        local[1][None],
+        sums[5:6, :hidden],
         g2[None],
-        wide[6][None],
+        sums[6:7],
     )
 
 

time: 976 us -> 817 us (0.84)
  Pallas kernels: 537 us -> 752 us
  waiting for transfers between devices: 173 us -> 0 us
  local copies, waits for them, and re-layouts: 144 us -> 53.6 us
  blocking collectives: 89.2 us -> 0 us
  between operations: 16.1 us -> 0.96 us
    pallas_call x1, Pallas kernels: 355 us -> 569 us  [on_device(): pl.pallas_call(functools.partial(backward_kernel, images, chunks, heads,...]
    unnamed x4 -> x0, waiting for transfers between devices: 130 us -> none
    psum x2 -> x0, blocking collectives: 89.2 us -> none  [the longest x1 70.1 us: on_device(): wide = lax.psum(small, ('dp', 'mp'))]
    unnamed x37 -> x12, local copies, waits for them, and re-layouts: 58.8 us -> 0.02 us
    all_gather x2 -> x0, waiting for transfers between devices: 42.7 us -> none  [the longest x1 42.7 us: on_device(): stack = lax.all_gather(part, 'dp', axis=1, tiled=True).astype(F32)]
    concatenate x1 -> x0, local copies, waits for them, and re-layouts: 30.9 us -> none  [on_device(): jnp.concatenate([g.astype(BF) for g in (gqkv, gout, g1[:hidden], g2[:hidd...]
    broadcast_in_dim x2, local copies, waits for them, and re-layouts: 5.16 us -> 18.5 us  [the longest x1 13.2 us: on_device(): g1[None]]
    all_gather x1 -> x0, local copies, waits for them, and re-layouts: 11.4 us -> none  [on_device(): stack = lax.all_gather(part, 'dp', axis=1, tiled=True).astype(F32)]
  transfers between devices with their start and end apart: 3 -> 0, of which waited for: 2 -> 0; matrix products, arithmetic and copies ran while one was open for 1% -> 0% of each run, Pallas kernels for 0% -> 0%
where the time goes in v2:
time: 817 us; the launch traced here: 812 us
  Pallas kernels  752 us (92%)
  local copies, waits for them, and re-layouts  53.6 us (7%)
    pallas_call x1, Pallas kernels, on_device(): pl.pallas_call(functools.partial(backward_kernel, images, chunks, heads,...  569 us
    pallas_call x1, Pallas kernels, on_device(): pl.pallas_call(functools.partial(forward_kernel, images, chunks, heads, l...  183 us

profile of v2, /device:TPU:0, one launch (start us, length us, event | category | flops | bytes accessed | tf_op | source)
XLA Modules:
  0.0 812.3 jit_solution(6614376444711939477)
XLA Ops:
  0.6 0.0 copy-start
  0.7 0.1 pad.39.clone
  0.7 0.9 slice_reduce_fusion.1
  1.6 0.1 stack.7
  1.7 0.1 stack.8
  1.8 0.1 pad_maximum_fusion
  1.9 0.6 pad_convert_fusion.1
  2.5 0.7 pad_convert_fusion
  3.2 1.4 concatenate.4.vec
  4.6 2.2 pad.35
  6.8 0.0 copy-start.1
  6.8 0.0 slice-start.2
  6.8 3.6 pad.36.w1
  10.3 0.0 copy-done
  10.3 0.0 slice-start.3
  10.4 1.7 pad.37.w2
  12.1 0.0 copy-done.1
  12.1 2.3 pad.34
  14.3 0.0 slice-done.2
  14.3 0.0 slice-done.3
  14.3 0.4 pad.30
  14.7 1.2 constant_dynamic-slice_fusion
  15.9 183.1 %layer_forward.1 = (bf16[3,192,1152]{2,1,0:T(8,128)(2,1)}, bf16[3,192,1152]{2,1,0:T(8,128)(2,1)}, bf16[3,768,1152]{2,1,0:T(8,128)(2,1)}, bf16[3,768,1536]{2,1,0:...) custom-call(bf16[3,192,1152]{2,1,0:T(8,128)(2,1)} %bitcast.43, ...), custom_call_target="tpu_custom_call" | custom-call | tf_op jit(solution)/shard_map/layer_forward/pallas_call | solution.py:997
  199.0 569.4 %layer_backward.1 = (bf16[3,3,4,64,1152]{4,3,2,1,0:T(8,128)(2,1)}, bf16[46,72,1152]{2,1,0:T(8,128)(2,1)}, f32[16,1152]{1,0:T(8,128)}) custom-call(bf16[3,192,1152]{2,1,0:T(8,128)(2,1)} %bitcast.44, bf16[3,3,64,1152]{3,2,1,0:T(8,128)(2,1)} %bitcast.60, f32[8,1152]{1,0:T(8,128)} %concatenate.4.vec, bf16[1536,1152]{1,0:T(8,128)(2,1)} %bitcast.42, ...), custom_call_target="tpu_custom_call" | custom-call | tf_op jit(solution)/shard_map/layer_backward/pallas_call | solution.py:1021
  768.4 0.0 slice-start
  768.4 5.3 slice_bitcast_fusion
  773.7 0.7 slice.56
  774.4 0.7 reshape.104
  775.1 1.4 slice.63
  776.5 1.7 fusion
  778.2 1.1 slice.58
  779.3 0.0 slice-start.1
  779.3 1.1 bitcast_convert_fusion
  780.5 2.3 slice.55
  782.8 2.2 convert_bitcast_fusion.1
  785.0 0.0 slice-done
  785.0 0.0 slice-done.1
  785.0 0.6 slice_convert_fusion
  785.6 13.3 %reshape.110 = f32[1,1076,1152]{2,0,1:T(1,128)} reshape(f32[1076,1152]{1,0:T(8,128)S(1)} %get-tuple-element.41) | data formatting | bytes 9916416 | tf_op jit(solution)/shard_map/broadcast_in_dim | solution.py:1097
  798.9 13.2 %reshape.109 = f32[1,1152,1076]{1,0,2:T(1,128)} reshape(f32[1152,1076]{0,1:T(8,128)S(1)} %get-tuple-element.42) | data formatting | bytes 9916416 | tf_op jit(solution)/shard_map/broadcast_in_dim | solution.py:1095
  (4 shorter events, 0.0 us)
Async XLA Ops:
  0.6 9.7 %copy-start = (bf16[1,1076,1152]{2,1,0:T(8,128)(2,1)S(1)}, bf16[1,1076,1152]{2,1,0:T(8,128)(2,1)}, u32[]{:S(2)}) copy-start(bf16[1,1076,1152]{2,1,0:T(8,128)(2,1)} %param.24) | copy-start | bytes 7437316
  6.8 5.3 copy-start.1
  6.8 7.5 slice-start.2
  10.3 4.0 slice-start.3
  768.4 16.6 %slice-start = ((s8[7630848]{0:T(1024)(128)(4,1)}), s8[3436544]{0:T(1024)(128)(4,1)S(1)}, s32[]{:S(2)}) async-start(s8[7630848]{0:T(1024)(128)(4,1)} %bitcast.49), calls=%async_computation | async-start | bytes 6873088
  779.3 5.7 slice-start.1

commit v3 on v2

--- a/solution.py
+++ b/solution.py
@@ -19,6 +19,7 @@
 HALF = CHUNK // 2
 VMEM_LIMIT = 67043328
 SKEW = 2
+AHEAD = 16
 SLOTS = 4
 PART_SLOTS = 8
 SUM_SLOTS = 8
@@ -409,7 +410,7 @@
     xin_i, a1_i, qkv_i, o_i, lse_i, a2_i, g_i, sl_i, h1_i,
     full_o, fin, sums_o,
     acc, small, gbqkv, obuf, fbuf, stage_buf, land_buf, sum_buf, mslot, dslot, sbuf, dbuf, xinb, a1b, qkvb, ob, lseb, a2b, gb, slb, h1b, dmb, dab, dqb, dkv, dob, outb,
-    part1, near1, out1, far1,
+    part1, near1, out1, far1, part2, near2, out2, far2,
     ssem, rsem, psend, precv, lsem, agsend, agrecv, msem, mrecv, dsem, drecv, zsend, zpart, zfinal, zpass, zkeep, pcredit, fcredit,
 ):
     spot = Spot(rows_mp)
@@ -444,14 +445,15 @@
             )
         ]
 
-    for ld in loads(0):
-        ld.start()
+    back_loads, front_loads = (7, 1, 2, 3, 0, 8), (4, 5, 6)
+    for n in back_loads:
+        loads(0)[n].start()
     enter(spot, dp_n)
     kinds = sem_kinds(rows_mp)
     gatm = Gather(dmb, ssem, rsem, kinds[0], spot)
     gata = Gather(dab, ssem, rsem, kinds[1], spot)
     red1 = Reduce(part1, near1, out1, far1, ssem, rsem, kinds[2], spot)
-    red2 = Reduce(part1, near1, out1, far1, ssem, rsem, kinds[3], spot)
+    red2 = Reduce(part2, near2, out2, far2, ssem, rsem, kinds[3], spot)
     every = range(chunks)
 
     acc[...] = jnp.zeros_like(acc)
@@ -508,7 +510,16 @@
 
         lax.fori_loop(0, a.shape[1] // step, tile, 0)
 
-    def attend(c):
+    def head_weights(base, a, b):
+        def head(n, carry):
+            cols = pl.ds(pl.multiple_of(n * HPAD, HPAD), HPAD)
+            start = base + n * HDIM
+            acc[pl.ds(pl.multiple_of(start, 8), HDIM)] += dot_tn(a[:, cols], b[...])[:HDIM]
+            return carry
+
+        lax.fori_loop(0, a.shape[1] // HPAD, head, 0)
+
+    def attend(c, between=()):
         rows = pl.ds(c * CHUNK, CHUNK)
         total = chunks * CHUNK
         valid = lax.broadcasted_iota(jnp.int32, (CHUNK, total), 1) < length
@@ -536,6 +547,9 @@
             else:
                 dkv[:, cq] += dk
                 dkv[:, ck] += dv
+            if h == heads // 2 - 1:
+                for action in between:
+                    action()
 
     def close():
         dk = (dkv[:, 0:hw] * scaling).astype(BF)
@@ -575,59 +589,300 @@
         load.wait()
         load_y.wait()
 
-    def image(i, carry):
-        ld = loads(i)
+    tall = stage_buf.shape[1]
+    units = fin.shape[0]
+    wide_units = 2 * pairs
+    right, left = lax.rem(z + 1, dp_n), lax.rem(z + dp_n - 1, dp_n)
+
+    def owner(u):
+        return dp_n // 2 - 1 + lax.rem(u, 2)
+
+    def send_copy(dst, u, side, recv):
+        slot = lax.rem(u, SLOTS)
+        return remote(stage_buf.at[slot], dst, zsend.at[slot, side], recv, {"dp": left if side else right})
+
+    def part_copy(u, side):
+        slot = lax.rem(u, PART_SLOTS)
+        return send_copy(land_buf.at[side, slot], u, side, zpart.at[side, slot])
+
+    def sum_copy(u, side):
+        slot = lax.rem(u, SUM_SLOTS)
+        return send_copy(sum_buf.at[slot], u, side, zfinal.at[slot])
+
+    def keep_copy(u):
+        slot = lax.rem(u, SLOTS)
+        return pltpu.make_async_copy(stage_buf.at[slot], fin.at[u], zsend.at[slot, 2])
+
+    def pass_copy(u, side):
+        slot = lax.rem(u, SUM_SLOTS)
+        view = sum_buf.at[slot]
+        return remote(view, view, zpass.at[slot], zfinal.at[slot], {"dp": left if side else right})
+
+    def write_copy(u):
+        slot = lax.rem(u, SUM_SLOTS)
+        return pltpu.make_async_copy(sum_buf.at[slot], fin.at[u], zkeep.at[slot])
+
+    def grant(sem, target):
+        pl.semaphore_signal(sem, inc=1, device_id={"dp": target}, device_id_type=MESH)
+
+    def sends(u, act):
+        mid = owner(u)
+
+        @pl.when((z <= mid) & (z < dp_n - 1))
+        def _():
+            act(0)
+
+        @pl.when((z >= mid) & (z > 0))
+        def _():
+            act(1)
+
+    def settle(u):
+        sends(u, lambda side: part_copy(u, side).wait_send())
+
+        @pl.when(z == owner(u))
+        def _():
+            keep_copy(u).wait()
+
+    def start_sum(copy, u, side):
+        @pl.when(u >= SUM_SLOTS)
+        def _():
+            pl.semaphore_wait(fcredit.at[side, lax.rem(u, 2)], 1)
+
+        copy.start()
+
+    def start_part(u, side):
+        @pl.when(u >= PART_SLOTS)
+        def _():
+            pl.semaphore_wait(pcredit.at[side, lax.rem(u, 2)], 1)
+
+        part_copy(u, side).start()
+
+    def reduce_unit(u, value):
+        mid = owner(u)
+        from_left = (z > 0) & (z <= mid)
+        from_right = (z < dp_n - 1) & (z >= mid)
+        for side, cond in ((0, from_left), (1, from_right)):
+
+            @pl.when(cond)
+            def _(side=side):
+                part_copy(u, side).wait_recv()
+
+            value = value + jnp.where(cond, land_buf[side, lax.rem(u, PART_SLOTS)].astype(F32), 0.0)
+
+        @pl.when(u >= SLOTS)
+        def _():
+            settle(u - SLOTS)
+
+        stage_buf[lax.rem(u, SLOTS)] = value.astype(BF)
+        for side, cond in ((0, from_left), (1, from_right)):
+
+            @pl.when(cond & (u + PART_SLOTS < units))
+            def _(side=side):
+                grant(pcredit.at[side, lax.rem(u, 2)], right if side else left)
+
+        @pl.when(z == mid)
+        def _():
+            keep_copy(u).start()
+            sends(u, lambda side: start_sum(sum_copy(u, side), u, side))
+
+        @pl.when(z != mid)
+        def _():
+            sends(u, lambda side: start_part(u, side))
+
+    def release(u):
+        mid = owner(u)
+        write_copy(u).wait()
+
+        @pl.when(((z < mid) & (z > 0)) | ((z > mid) & (z < dp_n - 1)))
+        def _():
+            pass_copy(u, 0).wait_send()
+
+        @pl.when((z < mid) & (u + SUM_SLOTS < units))
+        def _():
+            grant(fcredit.at[1, lax.rem(u, 2)], right)
+
+        @pl.when((z > mid) & (u + SUM_SLOTS < units))
+        def _():
+            grant(fcredit.at[0, lax.rem(u, 2)], left)
+
+    def spread_unit(u):
+        mid = owner(u)
+
+        @pl.when(z != mid)
+        def _():
+            sum_copy(u, 0).wait_recv()
+            write_copy(u).start()
+
+            @pl.when((z < mid) & (z > 0))
+            def _():
+                start_sum(pass_copy(u, 1), u, 1)
+
+            @pl.when((z > mid) & (z < dp_n - 1))
+            def _():
+                start_sum(pass_copy(u, 0), u, 0)
+
+            @pl.when(u >= 2)
+            def _():
+                release(u - 2)
+
+    half = dp_n // 2
+
+    def unit(t, carry):
+        mid = owner(t)
+        late = t - SKEW * (half + jnp.abs(z - mid))
+        now = t - SKEW * jnp.where(z < mid, z, jnp.where(z > mid, dp_n - 1 - z, half))
+
+        @pl.when((z != mid) & (late >= 0) & (late < units))
+        def _():
+            spread_unit(late)
+
+        @pl.when((now >= 0) & (now < wide_units))
+        def _():
+            start = now * tall + lax.div(now, pairs) * (hid - pairs * tall)
+            reduce_unit(now, acc[pl.ds(pl.multiple_of(start, 8), tall)])
+
+        @pl.when((now >= wide_units) & (now < units))
+        def _():
+            start = 2 * hid + (now - wide_units) * tall
+            reduce_unit(now, acc[pl.ds(pl.multiple_of(start, 8), tall)])
+
+        return carry
+
+    def slot(s, carry):
+        b, f = s - 1, s
+        has_b, has_f = b >= 0, f < images
+        back, front = pl.when(has_b), pl.when(has_f)
+        early, late = pl.when(has_f & (stage == 1)), pl.when(has_f & (stage == 0))
+
+        def chain(lo, hi):
+            @pl.when(b == images - 1)
+            def _():
+                lax.fori_loop(lo, hi, unit, 0)
+
+        @back
+        def _():
+            loads(b)[7].wait()
+            for c in every:
+                middle(b, c)
+            for c in every:
+                red1.drain(c)
+            weights(hid, slb, a2b, HPAD)
+
+        chain(0, 2)
+
+        @front
+        def _():
+            for n in front_loads:
+                loads(f)[n].start()
+
+        @back
+        def _():
+            for n in (0, 1, 2, 3, 8):
+                loads(b)[n].wait()
+            gata.forward(0)
+            attend(0, [functools.partial(gata.forward, c) for c in range(1, chunks - 1)])
+
+        @early
+        def _():
+            for c in every:
+                begin(f, c)
+
+        def pass_early():
+            @early
+            def _():
+                for c in range(chunks - 1):
+                    gatm.forward(c)
+
+        chain(2, 5)
+
+        @back
+        def _():
+            gata.forward(chunks - 1)
+            for c in range(1, chunks - 1):
+                attend(c)
+
+        chain(5, 8)
+
+        @back
+        def _():
+            attend(chunks - 1, [pass_early])
+
+        @pl.when(has_f & jnp.logical_not(has_b))
+        def _():
+            pass_early()
+
+        chain(8, 11)
+
+        @back
+        def _():
+            close()
+            for c in range(chunks - 1):
+                unproject(c)
+                if c >= 1:
+                    red2.cross(c - 1)
+            head_weights(2 * hid, ob, dab)
+            for c in every:
+                gata.drain(c)
+            unproject(chunks - 1)
+            red2.cross(chunks - 2)
+
+        @late
+        def _():
+            for c in every:
+                begin(f, c)
+            for c in range(chunks - 1):
+                gatm.forward(c)
+
+        @front
+        def _():
+            gatm.forward(chunks - 1)
+            for n in front_loads:
+                loads(f)[n].wait()
+
+        chain(11, 14)
         for c in every:
-            begin(i, c)
-        for c in every:
-            gatm.forward(c)
-        for n in (5, 6):
-            ld[n].wait()
-        for c in every:
-            feed(c)
-            if c >= 1:
-                red1.cross(c - 1)
-        for n in (0, 1, 2, 3, 4, 7, 8):
-            ld[n].wait()
-        middle(i, 0)
-        red1.cross(chunks - 1)
-        for c in range(1, chunks - 1):
-            middle(i, c)
-        for c in every:
-            gatm.drain(c)
-        weights(0, gb, dmb, HPAD)
-        middle(i, chunks - 1)
-        for c in every:
-            gata.forward(c)
-        weights(hid, slb, a2b, HPAD)
-        for c in every:
-            attend(c)
-        close()
-        for c in every:
-            red1.drain(c)
-        for c in every:
-            unproject(c)
-            if c >= 1:
-                red2.cross(c - 1)
-        red2.cross(chunks - 1)
-        for c in range(chunks - 1):
-            end(i, c)
-        weights(2 * hid, ob, dab, HPAD)
-        end(i, chunks - 1)
-        weights(2 * hid + hw, dqb, a1b, HPAD)
-        for c in every:
-            gata.drain(c)
-            red2.drain(c)
-            end_wait(i, c)
-
-        @pl.when(i + 1 < images)
-        def _():
-            for nx in loads(i + 1):
-                nx.start()
+
+            @front
+            def _():
+                feed(c)
+
+            @back
+            def _():
+                if c == 0:
+                    red2.cross(chunks - 1)
+                end(b, c)
+
+            @front
+            def _():
+                red1.cross(c)
+
+        @pl.when(has_b & (b + 1 < images))
+        def _():
+            loads(b + 1)[back_loads[0]].start()
+
+        @front
+        def _():
+            for c in every:
+                gatm.drain(c)
+            weights(0, gb, dmb, HPAD)
+
+        chain(14, AHEAD)
+
+        @back
+        def _():
+            head_weights(2 * hid + heads * HDIM, dqb, a1b)
+            for c in every:
+                red2.drain(c)
+                end_wait(b, c)
+
+        @pl.when(has_b & (b + 1 < images))
+        def _():
+            for n in back_loads[1:]:
+                loads(b + 1)[n].start()
 
         return carry
 
-    lax.fori_loop(0, images, image, 0)
+    lax.fori_loop(0, images + 1, slot, 0)
 
     def block(core, row):
         return full_o.at[:, :, core * rows_mp + row]
@@ -678,178 +933,18 @@
         dp_copy(j).start()
     dslot[z] = sbuf[...]
 
-    tall = stage_buf.shape[1]
-    units = fin.shape[0]
-    wide_units = 2 * pairs
-    right, left = lax.rem(z + 1, dp_n), lax.rem(z + dp_n - 1, dp_n)
-
-    def owner(u):
-        return dp_n // 2 - 1 + lax.rem(u, 2)
-
-    def send_copy(dst, u, side, recv):
-        slot = lax.rem(u, SLOTS)
-        return remote(stage_buf.at[slot], dst, zsend.at[slot, side], recv, {"dp": left if side else right})
-
-    def part_copy(u, side):
-        slot = lax.rem(u, PART_SLOTS)
-        return send_copy(land_buf.at[side, slot], u, side, zpart.at[side, slot])
-
-    def sum_copy(u, side):
-        slot = lax.rem(u, SUM_SLOTS)
-        return send_copy(sum_buf.at[slot], u, side, zfinal.at[slot])
-
-    def keep_copy(u):
-        slot = lax.rem(u, SLOTS)
-        return pltpu.make_async_copy(stage_buf.at[slot], fin.at[u], zsend.at[slot, 2])
-
-    def pass_copy(u, side):
-        slot = lax.rem(u, SUM_SLOTS)
-        view = sum_buf.at[slot]
-        return remote(view, view, zpass.at[slot], zfinal.at[slot], {"dp": left if side else right})
-
-    def write_copy(u):
-        slot = lax.rem(u, SUM_SLOTS)
-        return pltpu.make_async_copy(sum_buf.at[slot], fin.at[u], zkeep.at[slot])
-
-    def grant(sem, target):
-        pl.semaphore_signal(sem, inc=1, device_id={"dp": target}, device_id_type=MESH)
-
-    def sends(u, act):
-        mid = owner(u)
-
-        @pl.when((z <= mid) & (z < dp_n - 1))
-        def _():
-            act(0)
-
-        @pl.when((z >= mid) & (z > 0))
-        def _():
-            act(1)
-
-    def settle(u):
-        sends(u, lambda side: part_copy(u, side).wait_send())
-
-        @pl.when(z == owner(u))
-        def _():
-            keep_copy(u).wait()
-
-    def start_sum(copy, u, side):
-        @pl.when(u >= SUM_SLOTS)
-        def _():
-            pl.semaphore_wait(fcredit.at[side, lax.rem(u, 2)], 1)
-
-        copy.start()
-
-    def start_part(u, side):
-        @pl.when(u >= PART_SLOTS)
-        def _():
-            pl.semaphore_wait(pcredit.at[side, lax.rem(u, 2)], 1)
-
-        part_copy(u, side).start()
-
-    def reduce_unit(u, value):
-        mid = owner(u)
-        from_left = (z > 0) & (z <= mid)
-        from_right = (z < dp_n - 1) & (z >= mid)
-        for side, cond in ((0, from_left), (1, from_right)):
-
-            @pl.when(cond)
-            def _(side=side):
-                part_copy(u, side).wait_recv()
-
-            value = value + jnp.where(cond, land_buf[side, lax.rem(u, PART_SLOTS)].astype(F32), 0.0)
-
-        @pl.when(u >= SLOTS)
-        def _():
-            settle(u - SLOTS)
-
-        stage_buf[lax.rem(u, SLOTS)] = value.astype(BF)
-        for side, cond in ((0, from_left), (1, from_right)):
-
-            @pl.when(cond & (u + PART_SLOTS < units))
-            def _(side=side):
-                grant(pcredit.at[side, lax.rem(u, 2)], right if side else left)
-
-        @pl.when(z == mid)
-        def _():
-            keep_copy(u).start()
-            sends(u, lambda side: start_sum(sum_copy(u, side), u, side))
-
-        @pl.when(z != mid)
-        def _():
-            sends(u, lambda side: start_part(u, side))
-
-    def release(u):
-        mid = owner(u)
-        write_copy(u).wait()
-
-        @pl.when(((z < mid) & (z > 0)) | ((z > mid) & (z < dp_n - 1)))
-        def _():
-            pass_copy(u, 0).wait_send()
-
-        @pl.when((z < mid) & (u + SUM_SLOTS < units))
-        def _():
-            grant(fcredit.at[1, lax.rem(u, 2)], right)
-
-        @pl.when((z > mid) & (u + SUM_SLOTS < units))
-        def _():
-            grant(fcredit.at[0, lax.rem(u, 2)], left)
-
-    def spread_unit(u):
-        mid = owner(u)
-
-        @pl.when(z != mid)
-        def _():
-            sum_copy(u, 0).wait_recv()
-            write_copy(u).start()
-
-            @pl.when((z < mid) & (z > 0))
-            def _():
-                start_sum(pass_copy(u, 1), u, 1)
-
-            @pl.when((z > mid) & (z < dp_n - 1))
-            def _():
-                start_sum(pass_copy(u, 0), u, 0)
-
-            @pl.when(u >= 2)
-            def _():
-                release(u - 2)
-
-    half = dp_n // 2
-
-    def unit(t, carry):
-        mid = owner(t)
-        late = t - SKEW * (half + jnp.abs(z - mid))
-        now = t - SKEW * jnp.where(z < mid, z, jnp.where(z > mid, dp_n - 1 - z, half))
-
-        @pl.when((z != mid) & (late >= 0) & (late < units))
-        def _():
-            spread_unit(late)
-
-        @pl.when((now >= 0) & (now < wide_units))
-        def _():
-            start = now * tall + lax.div(now, pairs) * (hid - pairs * tall)
-            reduce_unit(now, acc[pl.ds(pl.multiple_of(start, 8), tall)])
-
-        @pl.when((now >= wide_units) & (now < units))
-        def _():
-            start = 2 * hid + (now - wide_units) * HPAD
-            reduce_unit(now, acc[pl.ds(pl.multiple_of(start, HPAD), tall)])
-
-        return carry
-
-    lax.fori_loop(0, 8, unit, 0)
     for j in range(1, dp_n):
         dp_copy(j).wait_recv()
     total = dslot[0]
     for j in range(1, dp_n):
         total = total + dslot[j]
     sums_o[...] = total
-    lax.fori_loop(8, 16, unit, 0)
+    lax.fori_loop(AHEAD, AHEAD + 4, unit, 0)
     for j in range(1, rows_mp):
         ag_far(j).wait_recv()
         ag_pass(j).start()
         ag_keep(j).start()
-    lax.fori_loop(16, units + SKEW * dp_n, unit, 0)
+    lax.fori_loop(AHEAD + 4, units + SKEW * dp_n, unit, 0)
 
     def last(t, carry):
         settle(t)
@@ -1028,7 +1123,7 @@
         in_specs=[anywhere()] * 2 + [vmem()] * 5 + [anywhere()] * 9,
         out_specs=[anywhere()] * 2 + [vmem()],
         scratch_shapes=[
-            pltpu.VMEM((2 * hid + 4 * hw, width), F32),
+            pltpu.VMEM((2 * hid + 4 * cols, width), F32),
             pltpu.VMEM((8, width), F32),
             pltpu.VMEM((1, 3 * hw), F32),
             pltpu.VMEM((images, chunks, piece, width), BF),
@@ -1049,7 +1144,7 @@
             pltpu.VMEM((total, 2 * hw), F32),
             pltpu.VMEM((CHUNK, hw), BF),
             pltpu.VMEM((own, width), BF),
-            *comm_scratch(chunks, width, rows_mp)[:4],
+            *comm_scratch(chunks, width, rows_mp),
             *sems(images, chunks, rows_mp),
             dma((2 * rows_mp - 1,)),
             dma((2 * rows_mp - 1,)),

time: 817 us -> 763 us (0.934)
  Pallas kernels: 752 us -> 699 us
    pallas_call x1, Pallas kernels: 569 us -> 516 us  [on_device(): pl.pallas_call(functools.partial(backward_kernel, images, chunks, heads,...]
where the time goes in v3:
time: 763 us; the launch traced here: 759 us
  Pallas kernels  699 us (92%)
  local copies, waits for them, and re-layouts  53.6 us (7%)
    pallas_call x1, Pallas kernels, on_device(): pl.pallas_call(functools.partial(backward_kernel, images, chunks, heads,...  516 us
    pallas_call x1, Pallas kernels, on_device(): pl.pallas_call(functools.partial(forward_kernel, images, chunks, heads, l...  183 us

profile of v3, /device:TPU:0, one launch (start us, length us, event | category | flops | bytes accessed | tf_op | source)
XLA Modules:
  0.0 759.2 jit_solution(1209304334451569148)
XLA Ops:
  0.6 0.0 copy-start
  0.7 0.1 pad.39.clone
  0.7 0.9 slice_reduce_fusion.1
  1.6 0.1 stack.7
  1.7 0.1 stack.8
  1.8 0.1 pad_maximum_fusion
  1.9 0.6 pad_convert_fusion.1
  2.5 0.7 pad_convert_fusion
  3.2 1.4 concatenate.4.vec
  4.6 2.2 pad.35
  6.8 0.0 copy-start.1
  6.8 0.0 slice-start.2
  6.8 3.6 pad.36.w1
  10.3 0.0 copy-done
  10.3 0.0 slice-start.3
  10.4 1.7 pad.37.w2
  12.1 0.0 copy-done.1
  12.1 2.3 pad.34
  14.3 0.0 slice-done.2
  14.3 0.0 slice-done.3
  14.3 0.4 pad.30
  14.7 1.2 constant_dynamic-slice_fusion
  15.9 183.1 %layer_forward.1 = (bf16[3,192,1152]{2,1,0:T(8,128)(2,1)}, bf16[3,192,1152]{2,1,0:T(8,128)(2,1)}, bf16[3,768,1152]{2,1,0:T(8,128)(2,1)}, bf16[3,768,1536]{2,1,0:...) custom-call(bf16[3,192,1152]{2,1,0:T(8,128)(2,1)} %bitcast.43, ...), custom_call_target="tpu_custom_call" | custom-call | tf_op jit(solution)/shard_map/layer_forward/pallas_call | solution.py:1092
  199.0 516.2 %layer_backward.1 = (bf16[3,3,4,64,1152]{4,3,2,1,0:T(8,128)(2,1)}, bf16[46,72,1152]{2,1,0:T(8,128)(2,1)}, f32[16,1152]{1,0:T(8,128)}) custom-call(bf16[3,192,1152]{2,1,0:T(8,128)(2,1)} %bitcast.44, bf16[3,3,64,1152]{3,2,1,0:T(8,128)(2,1)} %bitcast.60, f32[8,1152]{1,0:T(8,128)} %concatenate.4.vec, bf16[1536,1152]{1,0:T(8,128)(2,1)} %bitcast.42, ...), custom_call_target="tpu_custom_call" | custom-call | tf_op jit(solution)/shard_map/layer_backward/pallas_call | solution.py:1116
  715.2 0.0 slice-start
  715.2 5.3 slice_bitcast_fusion
  720.5 0.7 slice.56
  721.3 0.7 reshape.104
  721.9 1.4 slice.63
  723.3 1.7 fusion
  725.0 1.1 slice.58
  726.1 0.0 slice-start.1
  726.1 1.1 bitcast_convert_fusion
  727.3 2.3 slice.55
  729.6 2.2 convert_bitcast_fusion.1
  731.8 0.0 slice-done
  731.8 0.0 slice-done.1
  731.8 0.6 slice_convert_fusion
  732.4 13.3 %reshape.110 = f32[1,1076,1152]{2,0,1:T(1,128)} reshape(f32[1076,1152]{1,0:T(8,128)S(1)} %get-tuple-element.41) | data formatting | bytes 9916416 | tf_op jit(solution)/shard_map/broadcast_in_dim | solution.py:1192
  745.7 13.2 %reshape.109 = f32[1,1152,1076]{1,0,2:T(1,128)} reshape(f32[1152,1076]{0,1:T(8,128)S(1)} %get-tuple-element.42) | data formatting | bytes 9916416 | tf_op jit(solution)/shard_map/broadcast_in_dim | solution.py:1190
  (4 shorter events, 0.0 us)
Async XLA Ops:
  0.6 9.7 %copy-start = (bf16[1,1076,1152]{2,1,0:T(8,128)(2,1)S(1)}, bf16[1,1076,1152]{2,1,0:T(8,128)(2,1)}, u32[]{:S(2)}) copy-start(bf16[1,1076,1152]{2,1,0:T(8,128)(2,1)} %param.24) | copy-start | bytes 7437316
  6.8 5.3 copy-start.1
  6.8 7.5 slice-start.2
  10.3 4.0 slice-start.3
  715.2 16.6 %slice-start = ((s8[7630848]{0:T(1024)(128)(4,1)}), s8[3436544]{0:T(1024)(128)(4,1)S(1)}, s32[]{:S(2)}) async-start(s8[7630848]{0:T(1024)(128)(4,1)} %bitcast.49), calls=%async_computation | async-start | bytes 6873088
  726.1 5.7 slice-start.1

commit v4 on v3

--- a/solution.py
+++ b/solution.py
@@ -35,6 +35,10 @@
 
 def dot_tn(a, b):
     return lax.dot_general(a, b, (((0,), (0,)), ((), ())), preferred_element_type=F32)
+
+
+def tile_of(size):
+    return next(t for t in (512, 384, 256, HPAD) if size % t == 0)
 
 
 def col_sum(v):
@@ -408,8 +412,8 @@
     images, chunks, heads, length, scaling, rows_mp, dp_n, pairs,
     d_hbm, y_in, vec, wqkv, wout, w1, w2,
     xin_i, a1_i, qkv_i, o_i, lse_i, a2_i, g_i, sl_i, h1_i,
-    full_o, fin, sums_o,
-    acc, small, gbqkv, obuf, fbuf, stage_buf, land_buf, sum_buf, mslot, dslot, sbuf, dbuf, xinb, a1b, qkvb, ob, lseb, a2b, gb, slb, h1b, dmb, dab, dqb, dkv, dob, outb,
+    full_o, w2_o, w1_o, out_o, qkv_o, sums_o,
+    acc, small, gbqkv, obuf, fbuf, stage_buf, land_buf, sum_buf, wide_buf, mslot, dslot, sbuf, dbuf, xinb, a1b, qkvb, ob, lseb, a2b, gb, slb, h1b, dmb, dab, dqb, dkv, dob, outb,
     part1, near1, out1, far1, part2, near2, out2, far2,
     ssem, rsem, psend, precv, lsem, agsend, agrecv, msem, mrecv, dsem, drecv, zsend, zpart, zfinal, zpass, zkeep, pcredit, fcredit,
 ):
@@ -511,13 +515,15 @@
         lax.fori_loop(0, a.shape[1] // step, tile, 0)
 
     def head_weights(base, a, b):
-        def head(n, carry):
-            cols = pl.ds(pl.multiple_of(n * HPAD, HPAD), HPAD)
-            start = base + n * HDIM
-            acc[pl.ds(pl.multiple_of(start, 8), HDIM)] += dot_tn(a[:, cols], b[...])[:HDIM]
+        def group(n, carry):
+            cols = pl.ds(pl.multiple_of(n * hw, HPAD), hw)
+            part = dot_tn(a[:, cols], b[...])
+            for h in range(heads):
+                start = base + (n * heads + h) * HDIM
+                acc[pl.ds(pl.multiple_of(start, 8), HDIM)] += part[h * HPAD : h * HPAD + HDIM]
             return carry
 
-        lax.fori_loop(0, a.shape[1] // HPAD, head, 0)
+        lax.fori_loop(0, a.shape[1] // hw, group, 0)
 
     def attend(c, between=()):
         rows = pl.ds(c * CHUNK, CHUNK)
@@ -590,8 +596,8 @@
         load_y.wait()
 
     tall = stage_buf.shape[1]
-    units = fin.shape[0]
     wide_units = 2 * pairs
+    units = wide_units + 4 * heads
     right, left = lax.rem(z + 1, dp_n), lax.rem(z + dp_n - 1, dp_n)
 
     def owner(u):
@@ -609,19 +615,38 @@
         slot = lax.rem(u, SUM_SLOTS)
         return send_copy(sum_buf.at[slot], u, side, zfinal.at[slot])
 
-    def keep_copy(u):
-        slot = lax.rem(u, SLOTS)
-        return pltpu.make_async_copy(stage_buf.at[slot], fin.at[u], zsend.at[slot, 2])
+    def put(u, act):
+        slot = lax.rem(u, 2)
+        buf, sem = wide_buf.at[slot], zkeep.at[slot]
+
+        def rows(first):
+            return pl.ds(pl.multiple_of((u - first) * tall, 8), tall)
+
+        for ref, lo, hi in ((w2_o, 0, pairs), (w1_o, pairs, wide_units)):
+
+            @pl.when((u >= lo) & (u < hi))
+            def _(ref=ref, lo=lo):
+                act(pltpu.make_async_copy(buf, ref.at[rows(lo), 0], sem))
+
+        for ref, lo, hi in ((out_o, wide_units, wide_units + heads), (qkv_o, wide_units + heads, units)):
+
+            @pl.when((u >= lo) & (u < hi))
+            def _(ref=ref, lo=lo):
+                act(pltpu.make_async_copy(buf, ref.at[rows(lo)], sem))
+
+    def emit(u, value, settled):
+        @pl.when(settled)
+        def _():
+            put(u - 2, lambda copy: copy.wait())
+
+        wide_buf[lax.rem(u, 2)] = value.astype(F32)
+        put(u, lambda copy: copy.start())
 
     def pass_copy(u, side):
         slot = lax.rem(u, SUM_SLOTS)
         view = sum_buf.at[slot]
         return remote(view, view, zpass.at[slot], zfinal.at[slot], {"dp": left if side else right})
 
-    def write_copy(u):
-        slot = lax.rem(u, SUM_SLOTS)
-        return pltpu.make_async_copy(sum_buf.at[slot], fin.at[u], zkeep.at[slot])
-
     def grant(sem, target):
         pl.semaphore_signal(sem, inc=1, device_id={"dp": target}, device_id_type=MESH)
 
@@ -638,10 +663,6 @@
 
     def settle(u):
         sends(u, lambda side: part_copy(u, side).wait_send())
-
-        @pl.when(z == owner(u))
-        def _():
-            keep_copy(u).wait()
 
     def start_sum(copy, u, side):
         @pl.when(u >= SUM_SLOTS)
@@ -682,8 +703,8 @@
 
         @pl.when(z == mid)
         def _():
-            keep_copy(u).start()
             sends(u, lambda side: start_sum(sum_copy(u, side), u, side))
+            emit(u, stage_buf[lax.rem(u, SLOTS)], u >= 2)
 
         @pl.when(z != mid)
         def _():
@@ -691,7 +712,6 @@
 
     def release(u):
         mid = owner(u)
-        write_copy(u).wait()
 
         @pl.when(((z < mid) & (z > 0)) | ((z > mid) & (z < dp_n - 1)))
         def _():
@@ -711,7 +731,6 @@
         @pl.when(z != mid)
         def _():
             sum_copy(u, 0).wait_recv()
-            write_copy(u).start()
 
             @pl.when((z < mid) & (z > 0))
             def _():
@@ -720,6 +739,8 @@
             @pl.when((z > mid) & (z < dp_n - 1))
             def _():
                 start_sum(pass_copy(u, 0), u, 0)
+
+            emit(u, sum_buf[lax.rem(u, SUM_SLOTS)], u >= 2)
 
             @pl.when(u >= 2)
             def _():
@@ -766,7 +787,7 @@
                 middle(b, c)
             for c in every:
                 red1.drain(c)
-            weights(hid, slb, a2b, HPAD)
+            weights(hid, slb, a2b, tile_of(hid))
 
         chain(0, 2)
 
@@ -864,7 +885,7 @@
         def _():
             for c in every:
                 gatm.drain(c)
-            weights(0, gb, dmb, HPAD)
+            weights(0, gb, dmb, tile_of(hid))
 
         chain(14, AHEAD)
 
@@ -953,6 +974,8 @@
     lax.fori_loop(units - SLOTS, units, last, 0)
 
     def freed(u, carry):
+        put(u, lambda copy: copy.wait())
+
         @pl.when(z != owner(u))
         def _():
             release(u)
@@ -1111,17 +1134,19 @@
     dp_n = lax.axis_size("dp")
     tall_unit = HDIM
     pairs = -(-hidden // tall_unit)
-    units = 2 * pairs + 4 * heads
     dma = pltpu.SemaphoreType.DMA
-    full, fin, sums = pl.pallas_call(
+    full, g2, g1, gout, gqkv, sums = pl.pallas_call(
         functools.partial(backward_kernel, images, chunks, heads, length, scaling, rows_mp, dp_n, pairs),
         out_shape=[
             arr(images, chunks, 2 * rows_mp, piece, width),
-            arr(units, tall_unit, width),
+            arr(pairs * tall_unit, 1, width, dtype=F32),
+            arr(pairs * tall_unit, 1, width, dtype=F32),
+            arr(cols, width, dtype=F32),
+            arr(3 * cols, width, dtype=F32),
             arr(16, width, dtype=F32),
         ],
         in_specs=[anywhere()] * 2 + [vmem()] * 5 + [anywhere()] * 9,
-        out_specs=[anywhere()] * 2 + [vmem()],
+        out_specs=[anywhere()] * 5 + [vmem()],
         scratch_shapes=[
             pltpu.VMEM((2 * hid + 4 * cols, width), F32),
             pltpu.VMEM((8, width), F32),
@@ -1131,6 +1156,7 @@
             pltpu.VMEM((SLOTS, tall_unit, width), BF),
             pltpu.VMEM((2, PART_SLOTS, tall_unit, width), BF),
             pltpu.VMEM((SUM_SLOTS, tall_unit, width), BF),
+            pltpu.VMEM((2, tall_unit, width), F32),
             pltpu.VMEM((2 * rows_mp, 8, width), F32),
             pltpu.VMEM((dp_n, 16, width), F32),
             pltpu.VMEM((16, width), F32),
@@ -1167,14 +1193,7 @@
     )(mine, y_mine.reshape(images, chunks, piece, width), vec, wqkv, wout, w1, w2, *kept)
 
     section_out = full.reshape(images, total, width)[:, :length][None]
-    rows = fin.reshape(units * tall_unit, width)
-
-    def take(start, count):
-        return rows[start : start + count].astype(F32)
-
-    base = 2 * pairs * tall_unit
-    g2, g1 = take(0, hidden), take(pairs * tall_unit, hidden).T
-    gout, gqkv = take(base, cols), take(base + cols, 3 * cols)
+    g2, g1 = jnp.transpose(g2[:hidden], (1, 0, 2)), jnp.transpose(g1[:hidden], (1, 2, 0))
     gqkv = jnp.transpose(gqkv.reshape(3, cols, width), (2, 0, 1))
     gb = sums[8:10, :hw].reshape(2, heads, HPAD)[:, :, :HDIM].reshape(1, 2, cols)
     return (
@@ -1187,9 +1206,9 @@
         sums[2:3],
         sums[3:4],
         sums[4:5],
-        g1[None],
+        g1,
         sums[5:6, :hidden],
-        g2[None],
+        g2,
         sums[6:7],
     )
 

time: 763 us -> 731 us (0.958)
  local copies, waits for them, and re-layouts: 53.6 us -> 36.6 us
  Pallas kernels: 699 us -> 687 us
    broadcast_in_dim x2 -> x0, local copies, waits for them, and re-layouts: 26.5 us -> none  [the longest x1 13.3 us: on_device(): g2[None]]
    pallas_call x1, Pallas kernels: 516 us -> 504 us  [on_device(): pl.pallas_call(functools.partial(backward_kernel, images, chunks, heads,...]
    transpose x0 -> x1, local copies, waits for them, and re-layouts: none -> 9.86 us  [on_device(): jnp.transpose(g2[:hidden], (1, 0, 2))]
where the time goes in v4:
time: 731 us; the launch traced here: 726 us
  Pallas kernels  687 us (94%)
  local copies, waits for them, and re-layouts  36.6 us (5%)
    pallas_call x1, Pallas kernels, on_device(): pl.pallas_call(functools.partial(backward_kernel, images, chunks, heads,...  504 us
    pallas_call x1, Pallas kernels, on_device(): pl.pallas_call(functools.partial(forward_kernel, images, chunks, heads, l...  183 us

profile of v4, /device:TPU:0, one launch (start us, length us, event | category | flops | bytes accessed | tf_op | source)
XLA Modules:
  0.0 726.4 jit_solution(13348020791662643701)
XLA Ops:
  0.6 0.0 copy-start.1
  0.7 0.1 pad.39.clone
  0.7 0.9 slice_reduce_fusion.1
  1.6 0.1 stack.7
  1.7 0.1 stack.8
  1.8 0.1 pad_maximum_fusion
  1.9 0.6 pad_convert_fusion.1
  2.5 0.7 pad_convert_fusion
  3.2 1.4 concatenate.4.vec
  4.6 2.2 pad.35
  6.8 0.0 copy-start.2
  6.8 0.0 slice-start
  6.8 3.6 pad.36.w1
  10.4 0.0 copy-done.1
  10.4 0.0 slice-start.1
  10.4 1.7 pad.37.w2
  12.1 0.0 copy-done.2
  12.1 2.3 pad.34
  14.3 0.0 slice-done
  14.3 0.0 slice-done.1
  14.3 0.4 pad.30
  14.7 1.2 constant_dynamic-slice_fusion
  15.9 183.4 %layer_forward.1 = (bf16[3,192,1152]{2,1,0:T(8,128)(2,1)}, bf16[3,192,1152]{2,1,0:T(8,128)(2,1)}, bf16[3,768,1152]{2,1,0:T(8,128)(2,1)}, bf16[3,768,1536]{2,1,0:...) custom-call(bf16[3,192,1152]{2,1,0:T(8,128)(2,1)} %bitcast.36, ...), custom_call_target="tpu_custom_call" | custom-call | tf_op jit(solution)/shard_map/layer_forward/pallas_call | solution.py:1115
  199.3 504.0 %layer_backward.1 = (bf16[3,3,4,64,1152]{4,3,2,1,0:T(8,128)(2,1)}, f32[1080,1,1152]{2,1,0:T(1,128)}, f32[1080,1,1152]{2,1,0:T(1,128)}, f32[288,1152]{1,0:T(8,128...) custom-call(bf16[3,192,1152]{2,1,0:T(8,128)(2,1)} %bitcast.37, bf16[3,3,64,1152]{3,2,1,0:T(8,128)(2,1)} %bitcast.49, ...), custom_call_target="tpu_custom_call" | custom-call | tf_op jit(solution)/shard_map/layer_backward/pallas_call | solution.py:1138
  703.3 5.1 slice_bitcast_fusion
  708.4 0.7 slice.47
  709.2 0.7 reshape.87
  709.8 1.4 slice.53
  711.2 1.7 fusion
  712.9 0.0 copy-start
  712.9 9.9 %slice_bitcast_fusion.1 = (f32[1,1076,1152]{2,0,1:T(1,128)}, f32[1,1152,1076]{1,0,2:T(1,128)}) fusion(f32[1080,1,1152]{2,1,0:T(1,128)} %get-tuple-element.44, f32[1080,1,1152]{2,1,0:T(1,128)} %get-tuple-element.43), kind=kLoop, calls=%fused_computation.1 | loop fusion | bytes 19832832 | tf_op jit(solution)/shard_map/transpose | solution.py:1196
  722.8 0.0 copy-start.3
  722.8 0.0 copy-done
  722.8 1.9 copy.30
  724.7 0.3 copy-done.3
  725.0 1.1 copy.31
  (3 shorter events, 0.0 us)
Async XLA Ops:
  0.6 9.7 %copy-start.1 = (bf16[1,1076,1152]{2,1,0:T(8,128)(2,1)S(1)}, bf16[1,1076,1152]{2,1,0:T(8,128)(2,1)}, u32[]{:S(2)}) copy-start(bf16[1,1076,1152]{2,1,0:T(8,128)(2,1)} %param.24) | copy-start | bytes 7437316
  6.8 5.3 copy-start.2
  6.8 7.5 %slice-start = ((s8[5087232]{0:T(1024)(128)(4,1)}), s8[4194304]{0:T(1024)(128)(4,1)S(1)}, s32[]{:S(2)}) async-start(s8[5087232]{0:T(1024)(128)(4,1)} %bitcast.41), calls=%async_computation | async-start | bytes 8388608
  10.4 4.0 slice-start.1
  712.9 9.9 %copy-start = (f32[864,1152]{1,0:T(8,128)S(1)}, f32[864,1152]{1,0:T(8,128)}, u32[]{:S(2)}) copy-start(f32[864,1152]{1,0:T(8,128)} %get-tuple-element.41) | copy-start | bytes 11943940
  722.8 2.2 copy-start.3
